TPU v7x, 512 devices: a whole 4x8x8 slice. The times are simulated.
512 devices in a mesh: member: 32 (over z, x), wave: 16 (over y, core).
Axes of the slice: x: 4, y: 8, z: 8, core: 2. Of those that a mesh axis runs over, the one named last changes fastest.
Arguments:
- state: float32 [32, 128, 32, 640], P('member', 'wave'), may hold values from -6 to 6
- legendre: bfloat16 [128, 640, 640], P('wave'), may hold values from -0.25 to 0.25
- lat_weights: float32 [640], replicated, may hold values from 0.5 to 2
- region: int32 [4], replicated, may hold values from 0 to 2560, as said below
- sources: int32 [32], replicated, may hold values from 0 to 31, as said below
Outputs:
- new_states: float32 [32, 128, 32, 640], P('member', 'wave')
- scores: float32 [32], P('member')
Inputs may be any that keep to these rules, and one draw needn't show every extreme that they name: region[0] < region[1] bound the latitudes and region[2] < region[3] the longitudes of the region; each band covers at least half of its grid dimension; the longitude band ends at the last longitude, region[3] = 2560. `sources`: some member is the source of at least 8 slots.
All inputs are finite; a program needn't handle non-finite values.
Results may differ from a plain program's by a relative error of at most 0.0059.
Values may be sent and summed in bfloat16 or wider, within the bound.
No kernel may reach another device: no remote copies, remote signals or barrier semaphores. Data moves between devices by JAX's collectives and lax.ppermute only.
A program may use at most 128 MiB of HBM per device.

v0:
```python
import jax
import jax.numpy as jnp
from jax import lax
from jax.sharding import PartitionSpec as P

NLON = 2560


advect_rate = 2.0


def fourier_table(waves_total, points):
    wave_index = lax.broadcasted_iota(jnp.int32, (waves_total, points), 0)
    column_index = lax.broadcasted_iota(jnp.int32, (waves_total, points), 1)
    angles = (wave_index * column_index % points).astype(jnp.float32) * (2.0 * jnp.pi / points)
    return jnp.stack([jnp.cos(angles), -jnp.sin(angles)], axis=1).astype(jnp.bfloat16)


def on_device(state, legendre, lat_weights, region, sources):
    wave_count = lax.axis_size("wave")
    waves_local = legendre.shape[0]
    waves_total = waves_local * wave_count
    degrees = legendre.shape[1]
    latitudes = legendre.shape[2]
    lat_rows = latitudes // wave_count
    state_rows = state.shape[2]
    level_count = state_rows // 4
    fourier = fourier_table(waves_total, NLON)
    spectral = state[0]
    fourier_coef = jnp.einsum(
        "mrn,mnl->mrl", spectral.astype(jnp.bfloat16), legendre, preferred_element_type=jnp.float32
    )
    fourier_coef = fourier_coef.astype(jnp.bfloat16).reshape(
        waves_local, 2, 2 * level_count, latitudes
    )
    synthesis_scale = (2.0 * waves_total) ** (-0.5)
    gridded = synthesis_scale * jnp.einsum(
        "mckl,mcx->klx",
        lax.all_to_all(fourier_coef, "wave", split_axis=3, concat_axis=0, tiled=True),
        fourier,
        preferred_element_type=jnp.float32,
    )
    lat_start = lax.axis_index("wave") * lat_rows
    local_weights = lax.dynamic_slice_in_dim(lat_weights, lat_start, lat_rows)
    wind_grid = gridded[:level_count]
    temper_grid = gridded[level_count:]
    fluxes = (
        jnp.concatenate([0.5 * wind_grid * wind_grid, wind_grid * temper_grid], axis=0)
        * local_weights[None, :, None]
    )
    fluxes = fluxes.astype(jnp.bfloat16)
    lat_index = lat_start + lax.broadcasted_iota(jnp.int32, (lat_rows, 1), 0)
    lon_index = lax.broadcasted_iota(jnp.int32, (1, NLON), 1)
    in_region = (
        (lat_index >= region[0])
        & (lat_index < region[1])
        & (lon_index >= region[2])
        & (lon_index < region[3])
    )
    lowest = temper_grid[level_count - 1]
    region_part = jnp.sum(jnp.where(in_region, local_weights[:, None] * lowest * lowest, 0.0))
    region_total = lax.psum(region_part, "wave")
    every_lat = lax.broadcasted_iota(jnp.int32, (latitudes,), 0)
    lat_inside = (every_lat >= region[0]) & (every_lat < region[1])
    region_weight = jnp.sum(jnp.where(lat_inside, lat_weights, 0.0)) * (
        region[3] - region[2]
    ).astype(jnp.float32)
    scores = (region_total / region_weight).reshape(1)
    analysis_scale = NLON ** (-0.5)
    flux_coef = analysis_scale * jnp.einsum(
        "klx,mcx->mckl", fluxes, fourier, preferred_element_type=jnp.float32
    )
    flux_coef = flux_coef.astype(jnp.bfloat16)
    tendency = jnp.einsum(
        "mckl,mnl->mckn",
        lax.all_to_all(flux_coef, "wave", split_axis=0, concat_axis=3, tiled=True),
        legendre,
        preferred_element_type=jnp.float32,
    )
    wave_ids = lax.axis_index("wave") * waves_local + lax.broadcasted_iota(
        jnp.int32, (waves_local, 1, 1), 0
    )
    advection = advect_rate * wave_ids.astype(jnp.float32) / waves_total
    degree_ids = lax.broadcasted_iota(jnp.int32, (1, 1, degrees), 2).astype(jnp.float32)
    damping = 1.0 + ((degree_ids + 1.0) / degrees) ** 2
    spectral_split = spectral.reshape(waves_local, 2, 2 * level_count, degrees)
    real_part = (spectral_split[:, 0] + advection * tendency[:, 1]) / damping
    imag_part = (spectral_split[:, 1] - advection * tendency[:, 0]) / damping
    stepped = jnp.stack([real_part, imag_part], axis=1).reshape(1, waves_local, state_rows, degrees)
    source_member = sources[lax.axis_index("member")]
    shards = lax.all_gather(stepped, "member", axis=0, tiled=True)
    owners = lax.broadcasted_iota(jnp.int32, (shards.shape[0], 1, 1, 1), 0)
    cloned = jnp.sum(jnp.where(owners == source_member, shards, 0.0), axis=0, keepdims=True)
    return (cloned, scores)


def solution(mesh):
    in_specs = (P("member", "wave", None, None), P("wave", None, None), P(), P(), P())
    out_specs = (P("member", "wave", None, None), P("member"))
    return jax.shard_map(
        on_device, mesh=mesh, in_specs=in_specs, out_specs=out_specs, check_vma=False
    )
```

profile of v0, /device:TPU:1, one launch (start us, length us, event | category | flops | bytes accessed | tf_op | source)
XLA Modules:
  0.0 273.9 jit_solution(7735756794780903431)
XLA Ops:
  7.2 4.2 %convolution_convert_fusion = bf16[8,32,640]{2,1,0:T(8,128)(2,1)S(1)} fusion(bf16[8,640,640]{2,1,0:T(8,128)(2,1)} %param.6, f32[1,8,32,640]{3,2,1,0:T(8,128)} %param.5), kind=kOutput, calls=%fused_computation.24 | convolution fusion | flops 210042880 | bytes 7536640 | tf_op jit(solution)/shard_map/mrn,mnl->mrl/dot_general | solution.py:30
  11.4 3.3 %copy.16 = bf16[8,2,16,640]{2,1,0,3:T(2,128)(2,1)S(1)} copy(bf16[8,2,16,640]{3,2,1,0:T(8,128)(2,1)S(1)} %bitcast.65) | data formatting | bytes 655360 | tf_op jit(solution)/shard_map/reshape | solution.py:33
  14.7 3.4 %reshape.118 = bf16[16,2,5120]{2,1,0:T(2,128)(2,1)} reshape(bf16[640,8,2,16]{3,2,1,0:T(2,128)(2,1)S(1)} %bitcast.60) | data formatting | bytes 655360
  18.1 10.8 %all-to-all-start = ((bf16[16,2,5120]{2,1,0:T(2,128)(2,1)}), bf16[16,2,5120]{2,1,0:T(2,128)(2,1)}, u32[]{:S(2)}, u32[]{:S(2)}) async-start(bf16[16,2,5120]{2,1,0:T(2,128)(2,1)} %reshape.118), calls=%async_computation | async-start | bytes 655360 | tf_op jit(solution)/shard_map/all_to_all | solution.py:39
  29.0 6.1 %negate_convert_fusion = (bf16[128,1,2560]{2,0,1:T(8,128)(2,1)S(1)}, bf16[128,1,2560]{2,0,1:T(8,128)(2,1)}) fusion(), kind=kLoop, calls=%fused_computation.16 | loop fusion | flops 3932160 | bytes 1310720 | tf_op jit(solution)/shard_map/convert.1
  35.2 6.3 %all-to-all-done = bf16[16,2,5120]{2,1,0:T(2,128)(2,1)} async-done(((bf16[16,2,5120]{2,1,0:T(2,128)(2,1)}), bf16[16,2,5120]{2,1,0:T(2,128)(2,1)}, u32[]{:S(2)}, u32[]{:S(2)}) %all-to-all-start) | async-done | bytes 327712 | tf_op jit(solution)/shard_map/all_to_all | solution.py:39
  41.4 8.5 %reshape.119 = bf16[640,8,2,16]{3,2,1,0:T(2,128)(2,1)S(1)} reshape(bf16[16,2,5120]{2,1,0:T(2,128)(2,1)} %all-to-all-done) | data formatting | bytes 655360
  50.0 4.7 %copy.27 = bf16[8,2,16,16,40]{4,0,3,1,2:T(8,128)(2,1)} copy(bf16[8,2,16,16,40]{2,1,0,4,3:T(2,128)(2,1)S(1)} %bitcast.61) | data formatting | bytes 655360 | tf_op jit(solution)/shard_map/all_to_all | solution.py:39
  54.7 2.5 bitcast_multiply_fusion
  58.1 1.9 copy-done
  61.2 1.4 copy.20
  62.6 2.4 reshape.120
  65.0 3.6 %all-to-all-start.1 = ((bf16[16,2,5120]{2,1,0:T(2,128)(2,1)}), bf16[16,2,5120]{2,1,0:T(2,128)(2,1)S(1)}, u32[]{:S(2)}, u32[]{:S(2)}) async-start(bf16[16,2,5120]{2,1,0:T(2,128)(2,1)} %reshape.120), calls=%async_computation.1 | async-start | bytes 655360 | tf_op jit(solution)/shard_map/all_to_all | solution.py:76
  69.0 12.8 %all-to-all-done.1 = bf16[16,2,5120]{2,1,0:T(2,128)(2,1)S(1)} async-done(((bf16[16,2,5120]{2,1,0:T(2,128)(2,1)}), bf16[16,2,5120]{2,1,0:T(2,128)(2,1)S(1)}, u32[]{:S(2)}, u32[]{:S(2)}) %all-to-all-start.1) | async-done | bytes 327712 | tf_op jit(solution)/shard_map/all_to_all | solution.py:76
  81.7 1.6 reshape.121
  84.1 1.2 all_to_all.33
  85.3 4.9 %fusion.1 = f32[8,2,16,640]{3,2,1,0:T(8,128)S(1)} fusion(bf16[8,2,16,640]{3,2,1,0:T(8,128)(2,1)S(1)} %all_to_all.33, bf16[8,640,640]{2,1,0:T(8,128)(2,1)} %param.6), kind=kOutput, calls=%fused_computation.3 | convolution fusion | flops 209715200 | bytes 7536640 | tf_op jit(solution)/shard_map/mckl,mnl->mckn/dot_general | solution.py:74
  94.5 1.3 compare_and_fusion
  95.9 1.3 iota_compare_fusion
  97.1 1.9 select_reduce_fusion.1
  99.0 1.9 fusion.25
  101.5 23.4 %psum.7 = f32[]{:T(128)} all-reduce(f32[]{:T(128)} %fusion.25), channel_id=1, replica_groups=mesh['member'=32,'wave'=16] {'wave'}, use_global_device_ids=true, to_apply=%region_2.3 | all-reduce | flops 1 | bytes 8 | tf_op jit(solution)/shard_map/psum | solution.py:62
  125.5 130.8 %all-gather.2.cloned.1.call-done = f32[32,8,32,640]{3,2,1,0:T(8,128)} async-done(((f32[1,8,32,640]{3,2,1,0:T(8,128)}), f32[32,8,32,640]{3,2,1,0:T(8,128)}) %all-gather.2.cloned.1.call-update) | async-done | bytes 20971536 | tf_op jit(solution)/shard_map/all_gather | solution.py:91
  256.3 9.6 %select_reduce_fusion = f32[8,32,640]{2,1,0:T(8,128)} fusion(f32[32,8,32,640]{3,2,1,0:T(8,128)} %all-gather.2.cloned.1.call-done, pred[32]{0:T(512)(128)(4,1)S(1)} %iota_compare_fusion.4), kind=kLoop, calls=%fused_computation | loop fusion | flops 10321920 | bytes 21626912 | tf_op jit(solution)/shard_map/reduce_sum | solution.py:93
  (24 shorter events, 6.1 us)
Async XLA Ops:
  11.4 17.6 %copy-start.4 = (f32[640]{0:T(1024)S(1)}, f32[640]{0:T(1024)}, u32[]{:S(2)}) copy-start(f32[640]{0:T(1024)} %param.7) | copy-start | bytes 7684
  18.1 23.3 %all-to-all-start = ((bf16[16,2,5120]{2,1,0:T(2,128)(2,1)}), bf16[16,2,5120]{2,1,0:T(2,128)(2,1)}, u32[]{:S(2)}, u32[]{:S(2)}) async-start(bf16[16,2,5120]{2,1,0:T(2,128)(2,1)} %reshape.118), calls=%async_computation | async-start | bytes 655360 | tf_op jit(solution)/shard_map/all_to_all | solution.py:39
  57.2 2.8 %copy-start = (f32[16,40,2560]{2,1,0:T(8,128)}, f32[16,40,2560]{2,1,0:T(8,128)S(1)}, u32[]{:S(2)}) copy-start(f32[16,40,2560]{2,1,0:T(8,128)S(1)} %bitcast_multiply_fusion) | copy-start | bytes 19660804
  57.2 2.7 %copy-start.2 = (bf16[128,1,2560]{2,0,1:T(8,128)(2,1)S(1)}, bf16[128,1,2560]{2,0,1:T(8,128)(2,1)}, u32[]{:S(2)}) copy-start(bf16[128,1,2560]{2,0,1:T(8,128)(2,1)} %get-tuple-element.11) | copy-start | bytes 1966084
  65.0 16.7 %all-to-all-start.1 = ((bf16[16,2,5120]{2,1,0:T(2,128)(2,1)}), bf16[16,2,5120]{2,1,0:T(2,128)(2,1)S(1)}, u32[]{:S(2)}, u32[]{:S(2)}) async-start(bf16[16,2,5120]{2,1,0:T(2,128)(2,1)} %reshape.120), calls=%async_computation.1 | async-start | bytes 655360 | tf_op jit(solution)/shard_map/all_to_all | solution.py:76
  68.7 187.7 %all-gather.2.cloned.1.call-start = ((), (), s32[]{:S(2)}) async-start(), calls=%async_computation.2 | async-start | bytes 21626880 | tf_op jit(solution)/shard_map/all_gather | solution.py:91
  85.3 5.0 %copy-start.1 = (f32[1,8,32,640]{3,2,1,0:T(8,128)S(1)}, f32[1,8,32,640]{3,2,1,0:T(8,128)}, u32[]{:S(2)}) copy-start(f32[1,8,32,640]{3,2,1,0:T(8,128)} %param.5) | copy-start | bytes 1966084
  90.2 1.1 copy-start.3
  90.2 3.0 %copy-start.5 = (s32[32]{0:T(128)S(1)}, s32[32]{0:T(128)}, u32[]{:S(2)}) copy-start(s32[32]{0:T(128)} %param.9) | copy-start | bytes 388
Sparse Core Ops, SparseCore 0:
  91.5 164.8 all-gather.1
where the time goes:
time: 274 us
  waiting for transfers between devices  150 us (55%)
  local copies, waits for them, and re-layouts  30.6 us (11%)
  other arithmetic  24.6 us (9%)
  blocking collectives  23.4 us (9%)
  between operations  17.8 us (6%)
  starting transfers between devices  14.7 us (5%)
  matrix products  12.9 us (5%)
    all_gather x1, waiting for transfers between devices, on_device(): shards = lax.all_gather(stepped, 'member', axis=0, tiled=True)  131 us
    psum x1, blocking collectives, on_device(): region_total = lax.psum(region_part, 'wave')  23.4 us
    unnamed x16, local copies, waits for them, and re-layouts  17.9 us
    all_to_all x1, waiting for transfers between devices, on_device(): lax.all_to_all(flux_coef, 'wave', split_axis=0, concat_axis=3, tiled=True)  12.8 us
    all_to_all x1, starting transfers between devices, on_device(): lax.all_to_all(fourier_coef, 'wave', split_axis=3, concat_axis=0, tiled=T...  10.8 us
    reduce_sum x1, other arithmetic, on_device(): jnp.sum(jnp.where(owners == source_member, shards, 0.0), axis=0, keepdims...  9.6 us
    all_to_all x1, waiting for transfers between devices, on_device(): lax.all_to_all(fourier_coef, 'wave', split_axis=3, concat_axis=0, tiled=T...  6.27 us
    another operation x1, other arithmetic  6.15 us
  transfers between devices with their start and end apart: 3, of which 3 were waited for; matrix products, arithmetic and copies ran while one was open for 5% of the time, Pallas kernels for 0%

commit v1 on v0

v1 whole, which is shorter than its diff:
```python
import functools

import jax
import jax.numpy as jnp
from jax import lax
from jax.experimental import pallas as pl
from jax.experimental.pallas import tpu as pltpu
from jax.sharding import PartitionSpec as P

NLON = 2560
LANES = 128
COLUMNS = 256

advect_rate = 2.0


def fourier_table(waves_total, points):
    row = lax.broadcasted_iota(jnp.int32, (2 * waves_total, points), 0)
    column = lax.broadcasted_iota(jnp.int32, (2 * waves_total, points), 1)
    steps = ((row // 2) * column + (row % 2) * (points // 4)) % points
    angles = steps.astype(jnp.float32) * (2.0 * jnp.pi / points)
    return jnp.cos(angles).astype(jnp.bfloat16)


def put_rows(tiles_ref, where, values):
    for tile in range(tiles_ref.shape[0]):
        tiles_ref[tile, where, :] = values[:, tile * LANES : (tile + 1) * LANES]


def get_rows(tiles_ref, where):
    return jnp.concatenate([tiles_ref[tile, where, :] for tile in range(tiles_ref.shape[0])], axis=1)


def to_latitudes(levels, state_ref, legendre_ref, out_ref, rows_ref):
    step = pl.program_id(0)
    rows = state_ref.shape[1]
    first = pl.multiple_of(step * rows, rows)
    put_rows(
        rows_ref,
        pl.ds(first, rows),
        jnp.dot(
            state_ref[0].astype(jnp.bfloat16), legendre_ref[0], preferred_element_type=jnp.float32
        ),
    )

    @pl.when(step == pl.num_programs(0) - 1)
    def _():
        count = out_ref.shape[1]
        width = out_ref.shape[2]
        half = width // 2
        left = lax.broadcasted_iota(jnp.int32, (count, width), 1) < half
        for level in range(levels):
            wind = get_rows(rows_ref, pl.ds(level, count, stride=2 * levels))
            temper = get_rows(rows_ref, pl.ds(levels + level, count, stride=2 * levels))
            low = jnp.where(left, wind, pltpu.roll(temper, half, 1))
            high = jnp.where(left, pltpu.roll(wind, half, 1), temper)
            out_ref[2 * level] = low.astype(jnp.bfloat16)
            out_ref[2 * level + 1] = high.astype(jnp.bfloat16)


def on_grid(
    synthesis_scale,
    analysis_scale,
    info_ref,
    coef_ref,
    fourier_ref,
    weights_ref,
    out_ref,
    score_ref,
    turned_ref,
    total_ref,
    region_ref,
):
    points = fourier_ref.shape[1]
    lats = weights_ref.shape[0]
    turned_ref[...] = coef_ref[...].T
    total_ref[...] = jnp.zeros_like(total_ref)
    region_ref[...] = jnp.zeros_like(region_ref)
    weights = weights_ref[...]
    for part in range(points // COLUMNS):
        table = fourier_ref[:, part * COLUMNS : (part + 1) * COLUMNS]
        grid = synthesis_scale * jnp.dot(
            turned_ref[...], table, preferred_element_type=jnp.float32
        )
        wind, temper = grid[:lats], grid[lats:]
        weighted = wind * weights
        total_ref[:lats] += lax.dot_general(
            (0.5 * wind * weighted).astype(jnp.bfloat16),
            table,
            (((1,), (1,)), ((), ())),
            preferred_element_type=jnp.float32,
        )
        total_ref[lats:] += lax.dot_general(
            (weighted * temper).astype(jnp.bfloat16),
            table,
            (((1,), (1,)), ((), ())),
            preferred_element_type=jnp.float32,
        )
        column = part * COLUMNS + lax.broadcasted_iota(jnp.int32, (1, COLUMNS), 1)
        inside = (column >= info_ref[2]) & (column < info_ref[3])
        region_ref[...] += jnp.where(inside, temper * temper, 0.0)
    lat = info_ref[4] + lax.broadcasted_iota(jnp.int32, (lats, 1), 0)
    lat_inside = (lat >= info_ref[0]) & (lat < info_ref[1]) & (info_ref[5] == 1)
    score_ref[...] = jnp.sum(
        jnp.where(lat_inside, weights, 0.0) * jnp.sum(region_ref[...], axis=1, keepdims=True),
        axis=0,
        keepdims=True,
    )
    score = jnp.broadcast_to(score_ref[...], (out_ref.shape[0], LANES))
    high = score.astype(jnp.bfloat16).astype(jnp.float32)
    middle = (score - high).astype(jnp.bfloat16).astype(jnp.float32)
    low = score - high - middle
    lane = lax.broadcasted_iota(jnp.int32, score.shape, 1)
    parts = jnp.where(lane == 0, high, jnp.where(lane == 1, middle, jnp.where(lane == 2, low, 0.0)))
    out_ref[:, 2 * lats :] = parts.astype(jnp.bfloat16)
    out_ref[:, : 2 * lats] = (analysis_scale * total_ref[...]).T.astype(jnp.bfloat16)


def to_degrees(
    levels,
    waves_total,
    info_ref,
    coef_ref,
    legendre_ref,
    state_ref,
    lat_weights_ref,
    out_ref,
    scores_ref,
    wide_ref,
):
    step = pl.program_id(0)
    steps = pl.num_programs(0)
    owners, kept, _ = coef_ref.shape
    lats = lat_weights_ref.shape[1]
    half = lats // 2

    @pl.when(step == 0)
    def _():
        parts = jnp.zeros((1, LANES), jnp.float32)
        for owner in range(owners):
            put_rows(
                wide_ref,
                pl.ds(owner * kept, kept),
                coef_ref[owner][:, :lats].astype(jnp.float32),
            )
            parts += coef_ref[owner][0:1, lats:].astype(jnp.float32)
        lat = lax.broadcasted_iota(jnp.int32, (1, lats), 1)
        inside = (lat >= info_ref[0]) & (lat < info_ref[1])
        weight = jnp.sum(jnp.where(inside, lat_weights_ref[...], 0.0), axis=1, keepdims=True)
        columns = (info_ref[3] - info_ref[2]).astype(jnp.float32)
        scores_ref[...] = jnp.sum(parts, axis=1, keepdims=True) / (weight * columns)

    left = lax.broadcasted_iota(jnp.int32, (levels, lats), 1) < half
    rows = []
    for part in range(2):
        first = get_rows(wide_ref, pl.ds(2 * step + part, levels, stride=2 * kept))
        second = get_rows(wide_ref, pl.ds(kept + 2 * step + part, levels, stride=2 * kept))
        rows.append(jnp.where(left, first, pltpu.roll(second, half, 1)))
        rows.append(jnp.where(left, pltpu.roll(first, half, 1), second))
    tendency = lax.dot_general(
        jnp.concatenate(rows, axis=0).astype(jnp.bfloat16),
        legendre_ref[0],
        (((1,), (1,)), ((), ())),
        preferred_element_type=jnp.float32,
    )
    wave = (info_ref[6] * steps + step).astype(jnp.float32)
    advection = advect_rate * wave / waves_total
    degrees = tendency.shape[1]
    degree = lax.broadcasted_iota(jnp.int32, (1, degrees), 1).astype(jnp.float32)
    damping = 1.0 + ((degree + 1.0) / degrees) ** 2
    middle = 2 * levels
    out_ref[0, :middle] = (
        (state_ref[0, :middle] + advection * tendency[middle:]) / damping
    ).astype(jnp.bfloat16)
    out_ref[0, middle:] = (
        (state_ref[0, middle:] - advection * tendency[:middle]) / damping
    ).astype(jnp.bfloat16)


def pick(sources_ref, pieces_ref, out_ref):
    for slot in range(out_ref.shape[0]):
        out_ref[slot] = pieces_ref[sources_ref[slot]]


def on_device(state, legendre, lat_weights, region, sources):
    wave_count = lax.axis_size("wave")
    member_count = lax.axis_size("member")
    waves_local, degrees, latitudes = legendre.shape
    waves_total = waves_local * wave_count
    state_rows = state.shape[2]
    levels = state_rows // 4
    half = latitudes // 2
    kept = 2 * waves_local
    wave = lax.axis_index("wave")
    level = wave // 2
    lat_start = (wave % 2) * half
    spectral = state[0]
    vmem = functools.partial(pltpu.CompilerParams, vmem_limit_bytes=32 << 20)

    coef = pl.pallas_call(
        functools.partial(to_latitudes, levels),
        grid=(waves_local,),
        in_specs=[
            pl.BlockSpec((1, state_rows, degrees), lambda i: (i, 0, 0)),
            pl.BlockSpec((1, degrees, latitudes), lambda i: (i, 0, 0)),
        ],
        out_specs=pl.BlockSpec((wave_count, kept, latitudes), lambda i: (0, 0, 0)),
        out_shape=jax.ShapeDtypeStruct((wave_count, kept, latitudes), jnp.bfloat16),
        scratch_shapes=[pltpu.VMEM((latitudes // LANES, waves_local * state_rows, LANES), jnp.float32)],
        compiler_params=vmem(),
        name="to_latitudes",
    )(spectral, legendre)
    coef = lax.all_to_all(coef, "wave", split_axis=0, concat_axis=0, tiled=True)

    fourier = fourier_table(waves_total, NLON)
    info = jnp.concatenate(
        [
            region,
            jnp.stack([lat_start, (level == levels - 1).astype(jnp.int32), wave]).astype(jnp.int32),
        ]
    )
    weights = lax.dynamic_slice_in_dim(lat_weights, lat_start, half).reshape(half, 1)
    whole = pl.BlockSpec(memory_space=pltpu.VMEM)
    scalars = pl.BlockSpec(memory_space=pltpu.SMEM)
    width = latitudes + LANES
    flux_coef, _ = pl.pallas_call(
        functools.partial(on_grid, (2.0 * waves_total) ** (-0.5), NLON ** (-0.5)),
        in_specs=[scalars, whole, whole, whole],
        out_specs=[whole, whole],
        out_shape=[
            jax.ShapeDtypeStruct((2 * waves_total, width), jnp.bfloat16),
            jax.ShapeDtypeStruct((1, 1), jnp.float32),
        ],
        scratch_shapes=[
            pltpu.VMEM((latitudes, 2 * waves_total), jnp.bfloat16),
            pltpu.VMEM((latitudes, 2 * waves_total), jnp.float32),
            pltpu.VMEM((half, COLUMNS), jnp.float32),
        ],
        compiler_params=vmem(),
        name="on_grid",
    )(info, coef.reshape(2 * waves_total, latitudes), fourier, weights)
    flux_coef = lax.all_to_all(
        flux_coef.reshape(wave_count, kept, width), "wave", split_axis=0, concat_axis=0, tiled=True
    )

    stepped, scores = pl.pallas_call(
        functools.partial(to_degrees, levels, waves_total),
        grid=(waves_local,),
        in_specs=[
            scalars,
            pl.BlockSpec((wave_count, kept, width), lambda i: (0, 0, 0)),
            pl.BlockSpec((1, degrees, latitudes), lambda i: (i, 0, 0)),
            pl.BlockSpec((1, state_rows, degrees), lambda i: (i, 0, 0)),
            pl.BlockSpec((1, latitudes), lambda i: (0, 0)),
        ],
        out_specs=[
            pl.BlockSpec((1, state_rows, degrees), lambda i: (i, 0, 0)),
            pl.BlockSpec((1, 1), lambda i: (0, 0)),
        ],
        out_shape=[
            jax.ShapeDtypeStruct((waves_local, state_rows, degrees), jnp.bfloat16),
            jax.ShapeDtypeStruct((1, 1), jnp.float32),
        ],
        scratch_shapes=[pltpu.VMEM((latitudes // LANES, wave_count * kept, LANES), jnp.float32)],
        compiler_params=vmem(),
        name="to_degrees",
    )(info, flux_coef, legendre, spectral, lat_weights.reshape(1, latitudes))

    piece_rows = waves_local * state_rows // member_count
    pieces = lax.all_to_all(
        stepped.reshape(member_count, piece_rows, degrees),
        "member",
        split_axis=0,
        concat_axis=0,
        tiled=True,
    )
    picked = pl.pallas_call(
        pick,
        in_specs=[scalars, whole],
        out_specs=whole,
        out_shape=jax.ShapeDtypeStruct(pieces.shape, jnp.bfloat16),
        compiler_params=vmem(),
        name="pick",
    )(sources, pieces)
    cloned = lax.all_to_all(picked, "member", split_axis=0, concat_axis=0, tiled=True)
    cloned = cloned.reshape(1, waves_local, state_rows, degrees).astype(jnp.float32)
    return (cloned, scores.reshape(1))


def solution(mesh):
    in_specs = (P("member", "wave", None, None), P("wave", None, None), P(), P(), P())
    out_specs = (P("member", "wave", None, None), P("member"))
    return jax.shard_map(
        on_device, mesh=mesh, in_specs=in_specs, out_specs=out_specs, check_vma=False
    )
```

time: 274 us -> 105 us (0.38)
  waiting for transfers between devices: 150 us -> 16.4 us
  local copies, waits for them, and re-layouts: 30.6 us -> 6.99 us
  blocking collectives: 23.4 us -> 41.8 us
  between operations: 17.8 us -> 0.74 us
  matrix products: 12.9 us -> 0 us
  other arithmetic: 24.6 us -> 11.8 us
  Pallas kernels: 0 us -> 11.5 us
    all_gather x1 -> x0, waiting for transfers between devices: 131 us -> none  [on_device(): shards = lax.all_gather(stepped, 'member', axis=0, tiled=True)]
    all_to_all x0 -> x2, blocking collectives: none -> 41.8 us  [the longest x1 25.1 us: on_device(): lax.all_to_all(stepped.reshape(member_count, piece_rows, degrees), 'membe...]
    psum x1 -> x0, blocking collectives: 23.4 us -> none  [on_device(): region_total = lax.psum(region_part, 'wave')]
    reduce_sum x3 -> x0, other arithmetic: 13.4 us -> none  [the longest x1 9.6 us: on_device(): jnp.sum(jnp.where(owners == source_member, shards, 0.0), axis=0, keepdims...]
    dot_general x4 -> x0, matrix products: 12.9 us -> none  [the longest x1 4.95 us: on_device(): jnp.einsum('mckl,mnl->mckn', lax.all_to_all(flux_coef, 'wave', split_axis...]
    convert_element_type x0 -> x2, other arithmetic: none -> 11.7 us  [the longest x1 10.8 us: fourier_table(): return jnp.cos(angles).astype(jnp.bfloat16)]
    pallas_call x0 -> x4, Pallas kernels: none -> 11.5 us  [the longest x1 4.43 us: on_device(): pl.pallas_call(functools.partial(to_degrees, levels, waves_total), grid=(...]
    unnamed x16 -> x14, local copies, waits for them, and re-layouts: 17.9 us -> 6.82 us
  transfers between devices with their start and end apart: 3 -> 2, of which waited for: 3 -> 2; matrix products, arithmetic and copies ran while one was open for 5% -> 11% of each run, Pallas kernels for 0% -> 0%
where the time goes in v1:
time: 105 us
  blocking collectives  41.8 us (40%)
  waiting for transfers between devices  16.4 us (16%)
  starting transfers between devices  15.7 us (15%)
  other arithmetic  11.8 us (11%)
  Pallas kernels  11.5 us (11%)
  local copies, waits for them, and re-layouts  6.99 us (7%)
    all_to_all x1, blocking collectives, on_device(): lax.all_to_all(stepped.reshape(member_count, piece_rows, degrees), 'membe...  25.1 us
    all_to_all x1, blocking collectives, on_device(): lax.all_to_all(picked, 'member', split_axis=0, concat_axis=0, tiled=True)  16.7 us
    all_to_all x1, waiting for transfers between devices, on_device(): lax.all_to_all(flux_coef.reshape(wave_count, kept, width), 'wave', split_...  14.5 us
    convert_element_type x1, other arithmetic, fourier_table(): return jnp.cos(angles).astype(jnp.bfloat16)  10.8 us
    all_to_all x1, starting transfers between devices, on_device(): coef = lax.all_to_all(coef, 'wave', split_axis=0, concat_axis=0, tiled=True)  10.3 us
    unnamed x14, local copies, waits for them, and re-layouts  6.82 us
    all_to_all x1, starting transfers between devices, on_device(): lax.all_to_all(flux_coef.reshape(wave_count, kept, width), 'wave', split_...  5.4 us
    pallas_call x1, Pallas kernels, on_device(): pl.pallas_call(functools.partial(to_degrees, levels, waves_total), grid=(...  4.43 us
  transfers between devices with their start and end apart: 2, of which 2 were waited for; matrix products, arithmetic and copies ran while one was open for 11% of the time, Pallas kernels for 0%

profile of v1, /device:TPU:1, one launch (start us, length us, event | category | flops | bytes accessed | tf_op | source)
XLA Modules:
  0.0 104.9 jit_solution(12197030113406013068)
XLA Ops:
  0.6 0.0 copy-start
  0.6 2.9 %copy-done = bf16[8,640,640]{2,1,0:T(8,128)(2,1)S(1)} copy-done((bf16[8,640,640]{2,1,0:T(8,128)(2,1)S(1)}, bf16[8,640,640]{2,1,0:T(8,128)(2,1)}, u32[]{:S(2)}) %copy-start) | copy-done | bytes 6553624
  3.5 0.0 copy-start.2
  3.5 1.1 %copy-done.2 = f32[1,8,32,640]{3,2,1,0:T(8,128)S(1)} copy-done((f32[1,8,32,640]{3,2,1,0:T(8,128)S(1)}, f32[1,8,32,640]{3,2,1,0:T(8,128)}, u32[]{:S(2)}) %copy-start.2) | copy-done | bytes 655384
  4.6 3.1 %to_latitudes.1 = bf16[16,16,640]{2,1,0:T(8,128)(2,1)} custom-call(f32[8,32,640]{2,1,0:T(8,128)S(1)} %bitcast.10, bf16[8,640,640]{2,1,0:T(8,128)(2,1)S(1)} %copy-done), custom_call_target="tpu_custom_call" | custom-call | tf_op jit(solution)/shard_map/to_latitudes/pallas_call | solution.py:200
  7.7 10.3 %all-to-all-start = ((bf16[16,16,640]{2,1,0:T(8,128)(2,1)}), bf16[16,16,640]{2,1,0:T(8,128)(2,1)S(1)}, u32[]{:S(2)}, u32[]{:S(2)}) async-start(bf16[16,16,640]{2,1,0:T(8,128)(2,1)} %to_latitudes.1), calls=%async_computation | async-start | bytes 655360 | tf_op jit(solution)/shard_map/all_to_all | solution.py:213
  18.0 0.0 copy-done.5
  18.1 0.1 dynamic_slice.3
  18.1 0.1 reshape.45.weights_ref
  18.3 0.0 copy-done.6
  18.3 0.1 pad_add_fusion.info_ref
  18.3 10.8 %fusion.3.fourier_ref = bf16[256,2560]{1,0:T(8,128)(2,1)S(1)} fusion(s32[256]{0:T(256)S(1)} %get-tuple-element.9, s32[256]{0:T(256)S(1)} %get-tuple-element.12, s32[256]{0:T(256)S(1)} %get-tuple-element.8, s32[256]{0:T(256)S(1)} %get-tuple-element.13, pred[256]{0:T(512)(128)(4,1)S(1)} %get-tuple-element.10, pred[256]{0:T(512)(128)(4,1)S(1)} %get-tuple-element.11), kind=kLoop, calls=%fused_computation.4 | loop fusion | flops 9175040 | bytes 1315328 | tf_op jit(solution)/shard_map/convert_element_type | solution.py:22
  29.2 1.9 %all-to-all-done = bf16[16,16,640]{2,1,0:T(8,128)(2,1)S(1)} async-done(((bf16[16,16,640]{2,1,0:T(8,128)(2,1)}), bf16[16,16,640]{2,1,0:T(8,128)(2,1)S(1)}, u32[]{:S(2)}, u32[]{:S(2)}) %all-to-all-start) | async-done | bytes 327712 | tf_op jit(solution)/shard_map/all_to_all | solution.py:213
  31.0 3.4 %on_grid.1 = (bf16[256,768]{1,0:T(8,128)(2,1)}, f32[1,1]{1,0:T(1,128)}) custom-call(s32[7]{0:T(128)S(1)} %pad_add_fusion.info_ref, bf16[256,640]{1,0:T(8,128)(2,1)S(1)} %bitcast.12, bf16[256,2560]{1,0:T(8,128)(2,1)S(1)} %fusion.3.fourier_ref, f32[320,1]{1,0:T(8,128)S(1)} %reshape.45.weights_ref), custom_call_target="tpu_custom_call" | custom-call | tf_op jit(solution)/shard_map/on_grid/pallas_call | solution.py:226
  34.4 5.4 %all-to-all-start.1 = ((bf16[16,16,768]{2,1,0:T(8,128)(2,1)}), bf16[16,16,768]{2,1,0:T(8,128)(2,1)S(1)}, u32[]{:S(2)}, u32[]{:S(2)}) async-start(bf16[16,16,768]{2,1,0:T(8,128)(2,1)} %bitcast.5), calls=%async_computation.1 | async-start | bytes 786432 | tf_op jit(solution)/shard_map/all_to_all | solution.py:242
  39.8 14.5 %all-to-all-done.1.coef_ref = bf16[16,16,768]{2,1,0:T(8,128)(2,1)S(1)} async-done(((bf16[16,16,768]{2,1,0:T(8,128)(2,1)}), bf16[16,16,768]{2,1,0:T(8,128)(2,1)S(1)}, u32[]{:S(2)}, u32[]{:S(2)}) %all-to-all-start.1) | async-done | bytes 393248 | tf_op jit(solution)/shard_map/all_to_all | solution.py:242
  54.4 0.0 copy-done.3
  54.4 2.9 %copy-done.1 = bf16[8,640,640]{2,1,0:T(8,128)(2,1)S(1)} copy-done((bf16[8,640,640]{2,1,0:T(8,128)(2,1)S(1)}, bf16[8,640,640]{2,1,0:T(8,128)(2,1)}, u32[]{:S(2)}) %copy-start.1) | copy-done | bytes 6553624
  57.2 4.4 %to_degrees.1 = (bf16[8,32,640]{2,1,0:T(8,128)(2,1)S(1)}, f32[1,1]{1,0:T(1,128)}) custom-call(s32[7]{0:T(128)S(1)} %pad_add_fusion.info_ref, bf16[16,16,768]{2,1,0:T(8,128)(2,1)S(1)} %all-to-all-done.1.coef_ref, bf16[8,640,640]{2,1,0:T(8,128)(2,1)S(1)} %copy-done.1, f32[8,32,640]{2,1,0:T(8,128)S(1)} %bitcast.11, f32[1,640]{1,0:T(1,128)S(1)} %reshape.40.lat_weights_ref), custom_call_target="tpu_custom_call" | custom-call | tf_op jit(solution)/shard_map/to_degrees/pallas_call | solution.py:246
  61.7 25.1 %all_to_all.20.pieces_ref = bf16[32,8,640]{2,1,0:T(8,128)(2,1)S(1)} all-to-all(bf16[32,8,640]{2,1,0:T(8,128)(2,1)S(1)} %bitcast.13), channel_id=1, replica_groups=mesh['member'=32,'wave'=16] {'member'}, dimensions={0} | all-to-all | bytes 655360 | tf_op jit(solution)/shard_map/all_to_all | solution.py:270
  86.8 0.0 copy-done.4
  86.8 0.6 pick.1
  87.4 16.7 %all_to_all.21 = bf16[32,8,640]{2,1,0:T(8,128)(2,1)S(1)} all-to-all(bf16[32,8,640]{2,1,0:T(8,128)(2,1)S(1)} %pick.1), channel_id=1, replica_groups=mesh['member'=32,'wave'=16] {'member'}, dimensions={0} | all-to-all | bytes 655360 | tf_op jit(solution)/shard_map/all_to_all | solution.py:285
  104.1 0.9 convert.2
  (9 shorter events, 0.0 us)
Async XLA Ops:
  0.6 2.9 %copy-start = (bf16[8,640,640]{2,1,0:T(8,128)(2,1)S(1)}, bf16[8,640,640]{2,1,0:T(8,128)(2,1)}, u32[]{:S(2)}) copy-start(bf16[8,640,640]{2,1,0:T(8,128)(2,1)} %legendre_ref.3) | copy-start | bytes 19660804
  3.5 1.1 %copy-start.2 = (f32[1,8,32,640]{3,2,1,0:T(8,128)S(1)}, f32[1,8,32,640]{3,2,1,0:T(8,128)}, u32[]{:S(2)}) copy-start(f32[1,8,32,640]{3,2,1,0:T(8,128)} %param.5) | copy-start | bytes 1966084
  4.6 13.5 %copy-start.5 = (f32[640]{0:T(1024)S(1)}, f32[640]{0:T(1024)}, u32[]{:S(2)}) copy-start(f32[640]{0:T(1024)} %param.7) | copy-start | bytes 7684
  4.6 13.7 %copy-start.6 = (s32[4]{0:T(128)S(1)}, s32[4]{0:T(128)}, u32[]{:S(2)}) copy-start(s32[4]{0:T(128)} %param.8) | copy-start | bytes 52
  7.7 46.7 %copy-start.3 = (f32[1,8,32,640]{3,2,1,0:T(8,128)S(1)}, f32[1,8,32,640]{3,2,1,0:T(8,128)}, u32[]{:S(2)}) copy-start(f32[1,8,32,640]{3,2,1,0:T(8,128)} %param.5) | copy-start | bytes 1966084
  7.7 23.4 %all-to-all-start = ((bf16[16,16,640]{2,1,0:T(8,128)(2,1)}), bf16[16,16,640]{2,1,0:T(8,128)(2,1)S(1)}, u32[]{:S(2)}, u32[]{:S(2)}) async-start(bf16[16,16,640]{2,1,0:T(8,128)(2,1)} %to_latitudes.1), calls=%async_computation | async-start | bytes 655360 | tf_op jit(solution)/shard_map/all_to_all | solution.py:213
  34.4 19.9 %all-to-all-start.1 = ((bf16[16,16,768]{2,1,0:T(8,128)(2,1)}), bf16[16,16,768]{2,1,0:T(8,128)(2,1)S(1)}, u32[]{:S(2)}, u32[]{:S(2)}) async-start(bf16[16,16,768]{2,1,0:T(8,128)(2,1)} %bitcast.5), calls=%async_computation.1 | async-start | bytes 786432 | tf_op jit(solution)/shard_map/all_to_all | solution.py:242
  54.4 2.9 %copy-start.1 = (bf16[8,640,640]{2,1,0:T(8,128)(2,1)S(1)}, bf16[8,640,640]{2,1,0:T(8,128)(2,1)}, u32[]{:S(2)}) copy-start(bf16[8,640,640]{2,1,0:T(8,128)(2,1)} %legendre_ref.3) | copy-start | bytes 19660804
  57.2 29.5 %copy-start.4 = (s32[32]{0:T(128)S(1)}, s32[32]{0:T(128)}, u32[]{:S(2)}) copy-start(s32[32]{0:T(128)} %sources_ref.1) | copy-start | bytes 388

commit v2 on v1

v2 whole, which is shorter than its diff:
```python
import functools

import jax
import jax.numpy as jnp
from jax import lax
from jax.experimental import pallas as pl
from jax.experimental.pallas import tpu as pltpu
from jax.sharding import PartitionSpec as P

NLON = 2560
LANES = 128
COLUMNS = 256

advect_rate = 2.0


def fourier_table(waves_total, points):
    def angles(columns, stride, shift):
        row = lax.broadcasted_iota(jnp.int32, (2 * waves_total, columns), 0)
        column = lax.broadcasted_iota(jnp.int32, (2 * waves_total, columns), 1)
        steps = ((row >> 1) * (column * stride) + (row & 1) * shift) % points
        return steps.astype(jnp.float32) * (2.0 * jnp.pi / points)

    coarse = angles(points // LANES, LANES, points // 4)
    fine = angles(LANES, 1, 0)
    terms = lax.optimization_barrier(
        (jnp.cos(coarse), jnp.sin(coarse), jnp.cos(fine), jnp.sin(fine))
    )
    cos_coarse, sin_coarse = (term[:, :, None] for term in terms[:2])
    cos_fine, sin_fine = (term[:, None, :] for term in terms[2:])
    table = cos_coarse * cos_fine - sin_coarse * sin_fine
    return table.astype(jnp.bfloat16).reshape(2 * waves_total, points)


def put_rows(tiles_ref, where, values):
    for tile in range(tiles_ref.shape[0]):
        tiles_ref[tile, where, :] = values[:, tile * LANES : (tile + 1) * LANES]


def get_rows(tiles_ref, where):
    return jnp.concatenate([tiles_ref[tile, where, :] for tile in range(tiles_ref.shape[0])], axis=1)


def fetch(waves, *routes):
    copies = [
        [pltpu.make_async_copy(far.at[wave], near.at[wave], sems.at[wave]) for far, near, sems in routes]
        for wave in range(waves)
    ]
    for group in copies:
        for copy in group:
            copy.start()
    return copies


def to_latitudes(
    levels, state_hbm, legendre_hbm, out_ref, legendre_ref, state_ref, rows_ref, state_sems, legendre_sems
):
    waves, rows, _ = state_hbm.shape
    copies = fetch(waves, (state_hbm, state_ref, state_sems), (legendre_hbm, legendre_ref, legendre_sems))
    for wave in range(waves):
        for copy in copies[wave]:
            copy.wait()
        put_rows(
            rows_ref,
            pl.ds(wave * rows, rows),
            jnp.dot(
                state_ref[wave].astype(jnp.bfloat16),
                legendre_ref[wave],
                preferred_element_type=jnp.float32,
            ),
        )
    _, count, width = out_ref.shape
    half = width // 2
    left = lax.broadcasted_iota(jnp.int32, (count, width), 1) < half
    for level in range(levels):
        wind = get_rows(rows_ref, pl.ds(level, count, stride=2 * levels))
        temper = get_rows(rows_ref, pl.ds(levels + level, count, stride=2 * levels))
        low = jnp.where(left, wind, pltpu.roll(temper, half, 1))
        high = jnp.where(left, pltpu.roll(wind, half, 1), temper)
        out_ref[2 * level] = low.astype(jnp.bfloat16)
        out_ref[2 * level + 1] = high.astype(jnp.bfloat16)


def on_grid(
    synthesis_scale,
    analysis_scale,
    info_ref,
    coef_ref,
    fourier_ref,
    weights_ref,
    out_ref,
    score_ref,
    turned_ref,
    total_ref,
    region_ref,
):
    points = fourier_ref.shape[1]
    lats = weights_ref.shape[0]
    turned_ref[...] = coef_ref[...].T
    total_ref[...] = jnp.zeros_like(total_ref)
    region_ref[...] = jnp.zeros_like(region_ref)
    weights = weights_ref[...]
    for part in range(points // COLUMNS):
        table = fourier_ref[:, part * COLUMNS : (part + 1) * COLUMNS]
        grid = synthesis_scale * jnp.dot(
            turned_ref[...], table, preferred_element_type=jnp.float32
        )
        wind, temper = grid[:lats], grid[lats:]
        weighted = wind * weights
        total_ref[:lats] += lax.dot_general(
            (0.5 * wind * weighted).astype(jnp.bfloat16),
            table,
            (((1,), (1,)), ((), ())),
            preferred_element_type=jnp.float32,
        )
        total_ref[lats:] += lax.dot_general(
            (weighted * temper).astype(jnp.bfloat16),
            table,
            (((1,), (1,)), ((), ())),
            preferred_element_type=jnp.float32,
        )
        column = part * COLUMNS + lax.broadcasted_iota(jnp.int32, (1, COLUMNS), 1)
        inside = (column >= info_ref[2]) & (column < info_ref[3])
        region_ref[...] += jnp.where(inside, temper * temper, 0.0)
    lat = info_ref[4] + lax.broadcasted_iota(jnp.int32, (lats, 1), 0)
    lat_inside = (lat >= info_ref[0]) & (lat < info_ref[1]) & (info_ref[5] == 1)
    score_ref[...] = jnp.sum(
        jnp.where(lat_inside, weights, 0.0) * jnp.sum(region_ref[...], axis=1, keepdims=True),
        axis=0,
        keepdims=True,
    )
    score = jnp.broadcast_to(score_ref[...], (out_ref.shape[0], LANES))
    high = score.astype(jnp.bfloat16).astype(jnp.float32)
    middle = (score - high).astype(jnp.bfloat16).astype(jnp.float32)
    low = score - high - middle
    lane = lax.broadcasted_iota(jnp.int32, score.shape, 1)
    parts = jnp.where(lane == 0, high, jnp.where(lane == 1, middle, jnp.where(lane == 2, low, 0.0)))
    out_ref[:, 2 * lats :] = parts.astype(jnp.bfloat16)
    out_ref[:, : 2 * lats] = (analysis_scale * total_ref[...]).T.astype(jnp.bfloat16)


def to_degrees(
    levels,
    waves_total,
    info_ref,
    coef_ref,
    legendre_hbm,
    state_hbm,
    lat_weights_ref,
    out_ref,
    scores_ref,
    legendre_ref,
    state_ref,
    wide_ref,
    state_sems,
    legendre_sems,
):
    copies = fetch(
        state_hbm.shape[0], (state_hbm, state_ref, state_sems), (legendre_hbm, legendre_ref, legendre_sems)
    )
    owners, kept, _ = coef_ref.shape
    waves, degrees, lats = legendre_ref.shape
    half = lats // 2
    parts = jnp.zeros((1, LANES), jnp.float32)
    for owner in range(owners):
        put_rows(
            wide_ref,
            pl.ds(owner * kept, kept),
            coef_ref[owner][:, :lats].astype(jnp.float32),
        )
        parts += coef_ref[owner][0:1, lats:].astype(jnp.float32)
    lat = lax.broadcasted_iota(jnp.int32, (1, lats), 1)
    inside = (lat >= info_ref[0]) & (lat < info_ref[1])
    weight = jnp.sum(jnp.where(inside, lat_weights_ref[...], 0.0), axis=1, keepdims=True)
    columns = (info_ref[3] - info_ref[2]).astype(jnp.float32)
    scores_ref[...] = jnp.sum(parts, axis=1, keepdims=True) / (weight * columns)

    degree = lax.broadcasted_iota(jnp.int32, (1, degrees), 1).astype(jnp.float32)
    damping = 1.0 + ((degree + 1.0) / degrees) ** 2
    left = lax.broadcasted_iota(jnp.int32, (levels, lats), 1) < half
    middle = 2 * levels
    for wave in range(waves):
        rows = []
        for part in range(2):
            first = get_rows(wide_ref, pl.ds(2 * wave + part, levels, stride=2 * kept))
            second = get_rows(wide_ref, pl.ds(kept + 2 * wave + part, levels, stride=2 * kept))
            rows.append(jnp.where(left, first, pltpu.roll(second, half, 1)))
            rows.append(jnp.where(left, pltpu.roll(first, half, 1), second))
        for copy in copies[wave]:
            copy.wait()
        tendency = lax.dot_general(
            jnp.concatenate(rows, axis=0).astype(jnp.bfloat16),
            legendre_ref[wave],
            (((1,), (1,)), ((), ())),
            preferred_element_type=jnp.float32,
        )
        global_wave = (info_ref[6] * waves + wave).astype(jnp.float32)
        advection = advect_rate * global_wave / waves_total
        out_ref[wave, :middle] = (
            (state_ref[wave, :middle] + advection * tendency[middle:]) / damping
        ).astype(jnp.bfloat16)
        out_ref[wave, middle:] = (
            (state_ref[wave, middle:] - advection * tendency[:middle]) / damping
        ).astype(jnp.bfloat16)


def pick(sources_ref, pieces_ref, out_ref):
    for slot in range(out_ref.shape[0]):
        out_ref[slot] = pieces_ref[sources_ref[slot]]


def on_device(state, legendre, lat_weights, region, sources):
    wave_count = lax.axis_size("wave")
    member_count = lax.axis_size("member")
    waves_local, degrees, latitudes = legendre.shape
    waves_total = waves_local * wave_count
    state_rows = state.shape[2]
    levels = state_rows // 4
    half = latitudes // 2
    kept = 2 * waves_local
    wave = lax.axis_index("wave")
    level = wave // 2
    lat_start = (wave % 2) * half
    spectral = state[0]
    small = pltpu.CompilerParams(vmem_limit_bytes=32 << 20)

    whole = pl.BlockSpec(memory_space=pltpu.VMEM)
    scalars = pl.BlockSpec(memory_space=pltpu.SMEM)
    stay = pl.BlockSpec(memory_space=pltpu.HBM)
    large = pltpu.CompilerParams(vmem_limit_bytes=58 << 20)
    near = [
        pltpu.VMEM(legendre.shape, jnp.bfloat16),
        pltpu.VMEM(spectral.shape, jnp.float32),
    ]
    arrivals = [pltpu.SemaphoreType.DMA((waves_local,)), pltpu.SemaphoreType.DMA((waves_local,))]
    coef = pl.pallas_call(
        functools.partial(to_latitudes, levels),
        in_specs=[stay, stay],
        out_specs=whole,
        out_shape=jax.ShapeDtypeStruct((wave_count, kept, latitudes), jnp.bfloat16),
        scratch_shapes=[
            *near,
            pltpu.VMEM((latitudes // LANES, waves_local * state_rows, LANES), jnp.float32),
            *arrivals,
        ],
        compiler_params=large,
        name="to_latitudes",
    )(spectral, legendre)
    coef = lax.all_to_all(coef, "wave", split_axis=0, concat_axis=0, tiled=True)

    fourier = fourier_table(waves_total, NLON)
    info = jnp.concatenate(
        [
            region,
            jnp.stack([lat_start, (level == levels - 1).astype(jnp.int32), wave]).astype(jnp.int32),
        ]
    )
    weights = lax.dynamic_slice_in_dim(lat_weights, lat_start, half).reshape(half, 1)
    width = latitudes + LANES
    flux_coef, _ = pl.pallas_call(
        functools.partial(on_grid, (2.0 * waves_total) ** (-0.5), NLON ** (-0.5)),
        in_specs=[scalars, whole, whole, whole],
        out_specs=[whole, whole],
        out_shape=[
            jax.ShapeDtypeStruct((2 * waves_total, width), jnp.bfloat16),
            jax.ShapeDtypeStruct((1, 1), jnp.float32),
        ],
        scratch_shapes=[
            pltpu.VMEM((latitudes, 2 * waves_total), jnp.bfloat16),
            pltpu.VMEM((latitudes, 2 * waves_total), jnp.float32),
            pltpu.VMEM((half, COLUMNS), jnp.float32),
        ],
        compiler_params=small,
        name="on_grid",
    )(info, coef.reshape(2 * waves_total, latitudes), fourier, weights)
    lat_row, flux_coef = lax.optimization_barrier((lat_weights.reshape(1, latitudes), flux_coef))
    flux_coef = lax.all_to_all(
        flux_coef.reshape(wave_count, kept, width), "wave", split_axis=0, concat_axis=0, tiled=True
    )

    stepped, scores = pl.pallas_call(
        functools.partial(to_degrees, levels, waves_total),
        in_specs=[scalars, whole, stay, stay, whole],
        out_specs=[whole, whole],
        out_shape=[
            jax.ShapeDtypeStruct((waves_local, state_rows, degrees), jnp.bfloat16),
            jax.ShapeDtypeStruct((1, 1), jnp.float32),
        ],
        scratch_shapes=[
            *near,
            pltpu.VMEM((latitudes // LANES, wave_count * kept, LANES), jnp.float32),
            *arrivals,
        ],
        compiler_params=large,
        name="to_degrees",
    )(info, flux_coef, legendre, spectral, lat_row)

    piece_rows = waves_local * state_rows // member_count
    pieces = lax.all_to_all(
        stepped.reshape(member_count, piece_rows, degrees),
        "member",
        split_axis=0,
        concat_axis=0,
        tiled=True,
    )
    picked = pl.pallas_call(
        pick,
        in_specs=[scalars, whole],
        out_specs=whole,
        out_shape=jax.ShapeDtypeStruct(pieces.shape, jnp.bfloat16),
        compiler_params=small,
        name="pick",
    )(sources, pieces)
    cloned = lax.all_to_all(picked, "member", split_axis=0, concat_axis=0, tiled=True)
    cloned = cloned.reshape(1, waves_local, state_rows, degrees).astype(jnp.float32)
    return (cloned, scores.reshape(1))


def solution(mesh):
    in_specs = (P("member", "wave", None, None), P("wave", None, None), P(), P(), P())
    out_specs = (P("member", "wave", None, None), P("member"))
    return jax.shard_map(
        on_device, mesh=mesh, in_specs=in_specs, out_specs=out_specs, check_vma=False
    )
```

time: 105 us -> 98.1 us (0.934)
  blocking collectives: 41.8 us -> 58.5 us
  other arithmetic: 11.8 us -> 2.23 us
  waiting for transfers between devices: 16.4 us -> 10.1 us
  starting transfers between devices: 15.7 us -> 10.2 us
  local copies, waits for them, and re-layouts: 6.99 us -> 1.52 us
  Pallas kernels: 11.5 us -> 14.2 us
    all_to_all x0 -> x1, blocking collectives: none -> 17.3 us  [on_device(): lax.all_to_all(flux_coef.reshape(wave_count, kept, width), 'wave', split_...]
    all_to_all x1 -> x0, waiting for transfers between devices: 14.5 us -> none  [on_device(): lax.all_to_all(flux_coef.reshape(wave_count, kept, width), 'wave', split_...]
    convert_element_type x1, other arithmetic: 10.8 us -> 0.52 us  [fourier_table(): return table.astype(jnp.bfloat16).reshape(2 * waves_total, points)]
    all_to_all x1, waiting for transfers between devices: 1.87 us -> 10.1 us  [on_device(): coef = lax.all_to_all(coef, 'wave', split_axis=0, concat_axis=0, tiled=True)]
    unnamed x14 -> x8, local copies, waits for them, and re-layouts: 6.82 us -> 0.02 us
    all_to_all x1 -> x0, starting transfers between devices: 5.4 us -> none  [on_device(): lax.all_to_all(flux_coef.reshape(wave_count, kept, width), 'wave', split_...]
    pallas_call x2, Pallas kernels: 7.5 us -> 10.6 us  [the longest x1 6.26 us: on_device(): pl.pallas_call(functools.partial(to_degrees, levels, waves_total), in_spe...]
  transfers between devices with their start and end apart: 2 -> 1, of which waited for: 2 -> 1; matrix products, arithmetic and copies ran while one was open for 11% -> 3% of each run, Pallas kernels for 0% -> 0%
where the time goes in v2:
time: 98.1 us; the launch traced here: 97.6 us
  blocking collectives  58.5 us (60%)
  Pallas kernels  14.2 us (14%)
  starting transfers between devices  10.2 us (10%)
  waiting for transfers between devices  10.1 us (10%)
  other arithmetic  2.23 us (2%)
  local copies, waits for them, and re-layouts  1.52 us (2%)
    all_to_all x1, blocking collectives, on_device(): lax.all_to_all(stepped.reshape(member_count, piece_rows, degrees), 'membe...  25.3 us
    all_to_all x1, blocking collectives, on_device(): lax.all_to_all(flux_coef.reshape(wave_count, kept, width), 'wave', split_...  17.3 us
    all_to_all x1, blocking collectives, on_device(): lax.all_to_all(picked, 'member', split_axis=0, concat_axis=0, tiled=True)  15.8 us
    all_to_all x1, starting transfers between devices, on_device(): coef = lax.all_to_all(coef, 'wave', split_axis=0, concat_axis=0, tiled=True)  10.2 us
    all_to_all x1, waiting for transfers between devices, on_device(): coef = lax.all_to_all(coef, 'wave', split_axis=0, concat_axis=0, tiled=True)  10.1 us
    pallas_call x1, Pallas kernels, on_device(): pl.pallas_call(functools.partial(to_degrees, levels, waves_total), in_spe...  6.26 us
    pallas_call x1, Pallas kernels, on_device(): pl.pallas_call(functools.partial(to_latitudes, levels), in_specs=[stay, s...  4.38 us
    pallas_call x1, Pallas kernels, on_device(): pl.pallas_call(functools.partial(on_grid, (2.0 * waves_total) ** (-0.5),...  3.03 us
  transfers between devices with their start and end apart: 1, of which 1 were waited for; matrix products, arithmetic and copies ran while one was open for 3% of the time, Pallas kernels for 0%

profile of v2, /device:TPU:1, one launch (start us, length us, event | category | flops | bytes accessed | tf_op | source)
XLA Modules:
  0.0 97.6 jit_solution(4126213621594526718)
XLA Ops:
  0.6 0.0 copy-start.2
  0.6 4.4 %to_latitudes.1 = bf16[16,16,640]{2,1,0:T(8,128)(2,1)} custom-call(f32[8,32,640]{2,1,0:T(8,128)} %bitcast.14, bf16[8,640,640]{2,1,0:T(8,128)(2,1)} %legendre_hbm.3), custom_call_target="tpu_custom_call" | custom-call | tf_op jit(solution)/shard_map/to_latitudes/pallas_call | solution.py:236
  5.0 0.0 copy-start.3
  5.0 10.2 %all-to-all-start = ((bf16[16,16,640]{2,1,0:T(8,128)(2,1)}), bf16[16,16,640]{2,1,0:T(8,128)(2,1)S(1)}, u32[]{:S(2)}, u32[]{:S(2)}) async-start(bf16[16,16,640]{2,1,0:T(8,128)(2,1)} %to_latitudes.1), calls=%async_computation | async-start | bytes 655360 | tf_op jit(solution)/shard_map/all_to_all | solution.py:249
  15.3 0.2 fusion.11
  15.5 0.0 copy-done.2
  15.5 0.6 reshape.50.lat_weights_ref
  16.1 0.1 dynamic_slice.3
  16.1 0.1 reshape.58.weights_ref
  16.3 0.5 fusion.4
  16.8 0.5 subtract_convert_fusion
  17.4 0.8 copy.7.fourier_ref
  18.1 0.0 copy-done.3
  18.1 0.1 pad_add_fusion.info_ref
  18.2 10.1 %all-to-all-done = bf16[16,16,640]{2,1,0:T(8,128)(2,1)S(1)} async-done(((bf16[16,16,640]{2,1,0:T(8,128)(2,1)}), bf16[16,16,640]{2,1,0:T(8,128)(2,1)S(1)}, u32[]{:S(2)}, u32[]{:S(2)}) %all-to-all-start) | async-done | bytes 327712 | tf_op jit(solution)/shard_map/all_to_all | solution.py:249
  28.3 3.0 %on_grid.1 = (bf16[256,768]{1,0:T(8,128)(2,1)S(1)}, f32[1,1]{1,0:T(1,128)}) custom-call(s32[7]{0:T(128)S(1)} %pad_add_fusion.info_ref, bf16[256,640]{1,0:T(8,128)(2,1)S(1)} %bitcast.11, bf16[256,2560]{1,0:T(8,128)(2,1)S(1)} %copy.7.fourier_ref, f32[320,1]{1,0:T(8,128)S(1)} %reshape.58.weights_ref), custom_call_target="tpu_custom_call" | custom-call | tf_op jit(solution)/shard_map/on_grid/pallas_call | solution.py:260
  31.3 17.3 %all_to_all.20.coef_ref = bf16[16,16,768]{2,1,0:T(8,128)(2,1)} all-to-all(bf16[16,16,768]{2,1,0:T(8,128)(2,1)S(1)} %bitcast.12), channel_id=1, replica_groups=mesh['member'=32,'wave'=16] {'wave'}, dimensions={0} | all-to-all | bytes 786432 | tf_op jit(solution)/shard_map/all_to_all | solution.py:277
  48.7 0.0 copy-done
  48.7 6.3 %to_degrees.1 = (bf16[8,32,640]{2,1,0:T(8,128)(2,1)}, f32[1,1]{1,0:T(1,128)}) custom-call(s32[7]{0:T(128)} %copy-done, bf16[16,16,768]{2,1,0:T(8,128)(2,1)} %all_to_all.20.coef_ref, bf16[8,640,640]{2,1,0:T(8,128)(2,1)} %legendre_hbm.3, f32[8,32,640]{2,1,0:T(8,128)} %bitcast.15, f32[1,640]{1,0:T(1,128)} %reshape.50.lat_weights_ref), custom_call_target="tpu_custom_call" | custom-call | tf_op jit(solution)/shard_map/to_degrees/pallas_call | solution.py:281
  54.9 25.3 %all_to_all.21.pieces_ref = bf16[32,8,640]{2,1,0:T(8,128)(2,1)S(1)} all-to-all(bf16[32,8,640]{2,1,0:T(8,128)(2,1)} %bitcast.17), channel_id=1, replica_groups=mesh['member'=32,'wave'=16] {'member'}, dimensions={0} | all-to-all | bytes 655360 | tf_op jit(solution)/shard_map/all_to_all | solution.py:299
  80.3 0.0 copy-done.1
  80.3 0.6 pick.1
  80.9 15.8 %all_to_all.22 = bf16[32,8,640]{2,1,0:T(8,128)(2,1)S(1)} all-to-all(bf16[32,8,640]{2,1,0:T(8,128)(2,1)S(1)} %pick.1), channel_id=1, replica_groups=mesh['member'=32,'wave'=16] {'member'}, dimensions={0} | all-to-all | bytes 655360 | tf_op jit(solution)/shard_map/all_to_all | solution.py:314
  96.7 0.9 convert.2
  (4 shorter events, 0.0 us)
Async XLA Ops:
  0.6 14.9 %copy-start.2 = (f32[640]{0:T(1024)S(1)}, f32[640]{0:T(1024)}, u32[]{:S(2)}) copy-start(f32[640]{0:T(1024)} %param.7) | copy-start | bytes 7684
  5.0 13.1 %copy-start.3 = (s32[4]{0:T(128)S(1)}, s32[4]{0:T(128)}, u32[]{:S(2)}) copy-start(s32[4]{0:T(128)} %param.8) | copy-start | bytes 52
  5.0 23.3 %all-to-all-start = ((bf16[16,16,640]{2,1,0:T(8,128)(2,1)}), bf16[16,16,640]{2,1,0:T(8,128)(2,1)S(1)}, u32[]{:S(2)}, u32[]{:S(2)}) async-start(bf16[16,16,640]{2,1,0:T(8,128)(2,1)} %to_latitudes.1), calls=%async_computation | async-start | bytes 655360 | tf_op jit(solution)/shard_map/all_to_all | solution.py:249
  18.2 30.5 %copy-start = (s32[7]{0:T(128)}, s32[7]{0:T(128)S(1)}, u32[]{:S(2)}) copy-start(s32[7]{0:T(128)S(1)} %pad_add_fusion.info_ref) | copy-start | bytes 88
  48.7 31.6 %copy-start.1 = (s32[32]{0:T(128)S(1)}, s32[32]{0:T(128)}, u32[]{:S(2)}) copy-start(s32[32]{0:T(128)} %sources_ref.1) | copy-start | bytes 388

commit v3 on v2

v3 whole, which is shorter than its diff:
```python
import functools

import jax
import jax.numpy as jnp
from jax import lax
from jax.experimental import pallas as pl
from jax.experimental.pallas import tpu as pltpu
from jax.sharding import PartitionSpec as P

NLON = 2560
LANES = 128
COLUMNS = 256
AHEAD = 4

advect_rate = 2.0


def put_rows(tiles_ref, first_tile, where, values):
    for tile in range(values.shape[1] // LANES):
        tiles_ref[first_tile + tile, where, :] = values[:, tile * LANES : (tile + 1) * LANES]


def get_rows(tiles_ref, first_tile, tiles, where):
    return jnp.concatenate([tiles_ref[first_tile + tile, where, :] for tile in range(tiles)], axis=1)


def routes(waves, *pairs):
    copies = [
        [pltpu.make_async_copy(far.at[wave], near.at[wave], sems.at[wave]) for far, near, sems in pairs]
        for wave in range(waves)
    ]
    for group in copies[:AHEAD]:
        for copy in group:
            copy.start()
    return copies


def arrive(copies, wave):
    for copy in copies[wave]:
        copy.wait()
    for copy in copies[wave + AHEAD] if wave + AHEAD < len(copies) else ():
        copy.start()


def turns(row_steps, column_steps, shift, points):
    steps = row_steps * column_steps + shift
    steps = steps - jnp.floor(steps * (1.0 / points)) * points
    return steps * (2.0 * jnp.pi / points)


def to_latitudes(
    levels,
    state_hbm,
    legendre_hbm,
    out_ref,
    fourier_ref,
    legendre_ref,
    state_ref,
    rows_ref,
    state_sems,
    legendre_sems,
):
    waves, rows, _ = state_hbm.shape
    copies = routes(waves, (state_hbm, state_ref, state_sems), (legendre_hbm, legendre_ref, legendre_sems))
    table_rows, points = fourier_ref.shape
    total = table_rows // 2
    row = lax.broadcasted_iota(jnp.int32, (table_rows, LANES), 0)
    lane = lax.broadcasted_iota(jnp.int32, (table_rows, LANES), 1).astype(jnp.float32)
    quarter = jnp.where(row >= total, points // 4, 0).astype(jnp.float32)
    order = jnp.where(row >= total, row - total, row).astype(jnp.float32)
    coarse = turns(order, lane * LANES, quarter, points)
    fine = turns(order[:total], lane[:total], 0.0, points)
    cos_coarse, sin_coarse = jnp.cos(coarse), jnp.sin(coarse)
    cos_fine, sin_fine = jnp.cos(fine), jnp.sin(fine)
    tiles = points // LANES
    for wave in range(waves):
        arrive(copies, wave)
        product = jnp.dot(
            state_ref[wave].astype(jnp.bfloat16),
            legendre_ref[wave],
            preferred_element_type=jnp.float32,
        )
        put_rows(rows_ref, 0, pl.ds(wave * rows, rows), product)
        for tile in range(wave * tiles // waves, (wave + 1) * tiles // waves):
            for part in range(2):
                here = slice(part * total, (part + 1) * total)
                fourier_ref[here, tile * LANES : (tile + 1) * LANES] = (
                    cos_coarse[here, tile : tile + 1] * cos_fine
                    - sin_coarse[here, tile : tile + 1] * sin_fine
                ).astype(jnp.bfloat16)
    width = out_ref.shape[2] // 2
    half = width // 2
    span = width // LANES
    left = lax.broadcasted_iota(jnp.int32, (waves, width), 1) < half
    for level in range(levels):
        for part in range(2):
            first = 2 * levels * part + level
            wind = get_rows(rows_ref, 0, span, pl.ds(first, waves, stride=rows))
            temper = get_rows(rows_ref, 0, span, pl.ds(first + levels, waves, stride=rows))
            low = jnp.where(left, wind, pltpu.roll(temper, half, 1))
            high = jnp.where(left, pltpu.roll(wind, half, 1), temper)
            here = slice(part * width, (part + 1) * width)
            out_ref[2 * level, :, here] = low.astype(jnp.bfloat16)
            out_ref[2 * level + 1, :, here] = high.astype(jnp.bfloat16)


def on_grid(
    synthesis_scale,
    analysis_scale,
    levels,
    region_smem,
    coef_ref,
    fourier_ref,
    lat_weights_ref,
    out_ref,
    weights_ref,
    turned_ref,
    total_ref,
    region_ref,
):
    points = fourier_ref.shape[1]
    every = lat_weights_ref.shape[0]
    lats = every // 2
    waves = coef_ref.shape[0]
    position = lax.axis_index("wave")
    lat_start = pl.multiple_of((position % 2) * lats, 8)
    weights_ref[...] = jnp.broadcast_to(lat_weights_ref[...].reshape(1, every), (8, every)).T
    weights = weights_ref[pl.ds(lat_start, lats), 0:1]
    for part in range(2):
        turned_ref[:, part * waves : (part + 1) * waves] = coef_ref[:, part * every : (part + 1) * every].T
    total_ref[...] = jnp.zeros_like(total_ref)
    region_ref[...] = jnp.zeros_like(region_ref)
    for part in range(points // COLUMNS):
        table = fourier_ref[:, part * COLUMNS : (part + 1) * COLUMNS]
        grid = synthesis_scale * jnp.dot(
            turned_ref[...], table, preferred_element_type=jnp.float32
        )
        wind, temper = grid[:lats], grid[lats:]
        weighted = wind * weights
        total_ref[:lats] += lax.dot_general(
            (0.5 * wind * weighted).astype(jnp.bfloat16),
            table,
            (((1,), (1,)), ((), ())),
            preferred_element_type=jnp.float32,
        )
        total_ref[lats:] += lax.dot_general(
            (weighted * temper).astype(jnp.bfloat16),
            table,
            (((1,), (1,)), ((), ())),
            preferred_element_type=jnp.float32,
        )
        column = part * COLUMNS + lax.broadcasted_iota(jnp.int32, (1, COLUMNS), 1)
        inside = (column >= region_smem[2]) & (column < region_smem[3])
        region_ref[...] += jnp.where(inside, temper * temper, 0.0)
    lat = lat_start + lax.broadcasted_iota(jnp.int32, (lats, 1), 0)
    lowest = position // 2 == levels - 1
    lat_inside = (lat >= region_smem[0]) & (lat < region_smem[1]) & lowest
    score = jnp.sum(
        jnp.where(lat_inside, weights, 0.0) * jnp.sum(region_ref[...], axis=1, keepdims=True),
        axis=0,
        keepdims=True,
    )
    score = jnp.broadcast_to(score, (waves, LANES))
    high = score.astype(jnp.bfloat16).astype(jnp.float32)
    middle = (score - high).astype(jnp.bfloat16).astype(jnp.float32)
    low = score - high - middle
    lane = lax.broadcasted_iota(jnp.int32, score.shape, 1)
    parts = jnp.where(lane == 0, high, jnp.where(lane == 1, middle, jnp.where(lane == 2, low, 0.0)))
    out_ref[:, 2 * every :] = parts.astype(jnp.bfloat16)
    for part in range(2):
        out_ref[:, part * every : (part + 1) * every] = (
            (analysis_scale * total_ref[:, part * waves : (part + 1) * waves]).T.astype(jnp.bfloat16)
        )


def to_degrees(
    levels,
    waves_total,
    region_smem,
    coef_ref,
    legendre_ref,
    state_ref,
    lat_weights_ref,
    out_ref,
    scores_ref,
    wide_ref,
):
    waves, degrees, lats = legendre_ref.shape
    owners = coef_ref.shape[0]
    half = lats // 2
    span = lats // LANES
    parts = jnp.zeros((1, LANES), jnp.float32)
    for owner in range(owners):
        values = coef_ref[owner].astype(jnp.float32)
        put_rows(wide_ref, 0, pl.ds(owner * waves, waves), values[:, : 2 * lats])
        parts += values[0:1, 2 * lats :]
    lat = lax.broadcasted_iota(jnp.int32, (1, lats), 1)
    inside = (lat >= region_smem[0]) & (lat < region_smem[1])
    weight = jnp.sum(jnp.where(inside, lat_weights_ref[...].reshape(1, lats), 0.0), axis=1, keepdims=True)
    columns = (region_smem[3] - region_smem[2]).astype(jnp.float32)
    scores_ref[...] = jnp.sum(parts, axis=1, keepdims=True) / (weight * columns)

    position = lax.axis_index("wave")
    degree = lax.broadcasted_iota(jnp.int32, (1, degrees), 1).astype(jnp.float32)
    damping = 1.0 + ((degree + 1.0) / degrees) ** 2
    left = lax.broadcasted_iota(jnp.int32, (levels, lats), 1) < half
    middle = 2 * levels
    for wave in range(waves):
        rows = []
        for part in range(2):
            first = get_rows(wide_ref, part * span, span, pl.ds(wave, levels, stride=2 * waves))
            second = get_rows(wide_ref, part * span, span, pl.ds(waves + wave, levels, stride=2 * waves))
            rows.append(jnp.where(left, first, pltpu.roll(second, half, 1)))
            rows.append(jnp.where(left, pltpu.roll(first, half, 1), second))
        tendency = lax.dot_general(
            jnp.concatenate(rows, axis=0).astype(jnp.bfloat16),
            legendre_ref[wave],
            (((1,), (1,)), ((), ())),
            preferred_element_type=jnp.float32,
        )
        global_wave = (position * waves + wave).astype(jnp.float32)
        advection = advect_rate * global_wave / waves_total
        out_ref[wave, :middle] = (
            (state_ref[wave, :middle] + advection * tendency[middle:]) / damping
        ).astype(jnp.bfloat16)
        out_ref[wave, middle:] = (
            (state_ref[wave, middle:] - advection * tendency[:middle]) / damping
        ).astype(jnp.bfloat16)


def pick(sources_smem, pieces_ref, out_ref):
    for slot in range(out_ref.shape[0]):
        out_ref[slot] = pieces_ref[sources_smem[slot]]


def on_device(state, legendre, lat_weights, region, sources):
    wave_count = lax.axis_size("wave")
    member_count = lax.axis_size("member")
    waves_local, degrees, latitudes = legendre.shape
    waves_total = waves_local * wave_count
    state_rows = state.shape[2]
    levels = state_rows // 4
    half = latitudes // 2
    spectral = state[0]
    lat_row = lat_weights
    whole = pl.BlockSpec(memory_space=pltpu.VMEM)
    scalars = pl.BlockSpec(memory_space=pltpu.SMEM)
    stay = pl.BlockSpec(memory_space=pltpu.HBM)
    small = pltpu.CompilerParams(vmem_limit_bytes=24 << 20)
    near = [
        pltpu.VMEM(legendre.shape, jnp.bfloat16),
        pltpu.VMEM(spectral.shape, jnp.float32),
    ]
    arrivals = [pltpu.SemaphoreType.DMA((waves_local,)), pltpu.SemaphoreType.DMA((waves_local,))]

    coef, fourier = pl.pallas_call(
        functools.partial(to_latitudes, levels),
        in_specs=[stay, stay],
        out_specs=[whole, whole],
        out_shape=[
            jax.ShapeDtypeStruct((wave_count, waves_local, 2 * latitudes), jnp.bfloat16),
            pltpu.VMEM((2 * waves_total, NLON), jnp.bfloat16),
        ],
        scratch_shapes=[
            *near,
            pltpu.VMEM((latitudes // LANES, waves_local * state_rows, LANES), jnp.float32),
            *arrivals,
        ],
        compiler_params=pltpu.CompilerParams(vmem_limit_bytes=52 << 20),
        name="to_latitudes",
    )(spectral, legendre)
    coef = lax.all_to_all(coef, "wave", split_axis=0, concat_axis=0, tiled=True)

    width = 2 * latitudes + LANES
    flux_coef = pl.pallas_call(
        functools.partial(on_grid, (2.0 * waves_total) ** (-0.5), NLON ** (-0.5), levels),
        in_specs=[scalars, whole, whole, whole],
        out_specs=whole,
        out_shape=jax.ShapeDtypeStruct((waves_total, width), jnp.bfloat16),
        scratch_shapes=[
            pltpu.VMEM((latitudes, 8), jnp.float32),
            pltpu.VMEM((latitudes, 2 * waves_total), jnp.bfloat16),
            pltpu.VMEM((latitudes, 2 * waves_total), jnp.float32),
            pltpu.VMEM((half, COLUMNS), jnp.float32),
        ],
        compiler_params=small,
        name="on_grid",
    )(region, coef.reshape(waves_total, 2 * latitudes), fourier, lat_row)
    flux_coef = lax.all_to_all(
        flux_coef.reshape(wave_count, waves_local, width), "wave", split_axis=0, concat_axis=0, tiled=True
    )

    stepped, scores = pl.pallas_call(
        functools.partial(to_degrees, levels, waves_total),
        in_specs=[scalars, whole, whole, whole, whole],
        out_specs=[whole, whole],
        out_shape=[
            jax.ShapeDtypeStruct((waves_local, state_rows, degrees), jnp.bfloat16),
            jax.ShapeDtypeStruct((1, 1), jnp.float32),
        ],
        scratch_shapes=[
            pltpu.VMEM((2 * latitudes // LANES, wave_count * waves_local, LANES), jnp.float32)
        ],
        compiler_params=small,
        name="to_degrees",
    )(region, flux_coef, legendre, spectral, lat_row)

    piece_rows = waves_local * state_rows // member_count
    pieces = lax.all_to_all(
        stepped.reshape(member_count, piece_rows, degrees),
        "member",
        split_axis=0,
        concat_axis=0,
        tiled=True,
    )
    picked = pl.pallas_call(
        pick,
        in_specs=[scalars, whole],
        out_specs=whole,
        out_shape=jax.ShapeDtypeStruct(pieces.shape, jnp.bfloat16),
        compiler_params=small,
        name="pick",
    )(sources, pieces)
    cloned = lax.all_to_all(picked, "member", split_axis=0, concat_axis=0, tiled=True)
    cloned = cloned.reshape(1, waves_local, state_rows, degrees).astype(jnp.float32)
    return (cloned, scores.reshape(1))


def solution(mesh):
    in_specs = (P("member", "wave", None, None), P("wave", None, None), P(), P(), P())
    out_specs = (P("member", "wave", None, None), P("member"))
    return jax.shard_map(
        on_device, mesh=mesh, in_specs=in_specs, out_specs=out_specs, check_vma=False
    )
```

time: 98.1 us -> 94.7 us (0.965)
  blocking collectives: 58.5 us -> 81.3 us
  starting transfers between devices: 10.2 us -> 0 us
  waiting for transfers between devices: 10.1 us -> 0 us
  Pallas kernels: 14.2 us -> 11.6 us
  local copies, waits for them, and re-layouts: 1.52 us -> 0.02 us
  other arithmetic: 2.23 us -> 0.89 us
    all_to_all x1 -> x2, blocking collectives: 17.3 us -> 39 us  [the longest x1 22.3 us: on_device(): coef = lax.all_to_all(coef, 'wave', split_axis=0, concat_axis=0, tiled=True)]
    all_to_all x1 -> x0, starting transfers between devices: 10.2 us -> none  [on_device(): coef = lax.all_to_all(coef, 'wave', split_axis=0, concat_axis=0, tiled=True)]
    all_to_all x1 -> x0, waiting for transfers between devices: 10.1 us -> none  [on_device(): coef = lax.all_to_all(coef, 'wave', split_axis=0, concat_axis=0, tiled=True)]
    pallas_call x1, Pallas kernels: 6.26 us -> 3.1 us  [on_device(): pl.pallas_call(functools.partial(to_degrees, levels, waves_total), in_spe...]
  transfers between devices with their start and end apart: 1 -> 0, of which waited for: 1 -> 0; matrix products, arithmetic and copies ran while one was open for 3% -> 0% of each run, Pallas kernels for 0% -> 0%
where the time goes in v3:
time: 94.7 us; the launch traced here: 94.5 us
  blocking collectives  81.3 us (86%)
  Pallas kernels  11.6 us (12%)
    all_to_all x1, blocking collectives, on_device(): lax.all_to_all(stepped.reshape(member_count, piece_rows, degrees), 'membe...  25.8 us
    all_to_all x1, blocking collectives, on_device(): coef = lax.all_to_all(coef, 'wave', split_axis=0, concat_axis=0, tiled=True)  22.3 us
    all_to_all x1, blocking collectives, on_device(): lax.all_to_all(flux_coef.reshape(wave_count, waves_local, width), 'wave',...  16.6 us
    all_to_all x1, blocking collectives, on_device(): lax.all_to_all(picked, 'member', split_axis=0, concat_axis=0, tiled=True)  16.5 us
    pallas_call x1, Pallas kernels, on_device(): pl.pallas_call(functools.partial(to_latitudes, levels), in_specs=[stay, s...  4.97 us
    pallas_call x1, Pallas kernels, on_device(): pl.pallas_call(functools.partial(to_degrees, levels, waves_total), in_spe...  3.1 us
    pallas_call x1, Pallas kernels, on_device(): pl.pallas_call(functools.partial(on_grid, (2.0 * waves_total) ** (-0.5),...  2.94 us

profile of v3, /device:TPU:1, one launch (start us, length us, event | category | flops | bytes accessed | tf_op | source)
XLA Modules:
  0.0 94.5 jit_solution(7283606669765431871)
XLA Ops:
  0.6 0.0 copy-start
  0.6 0.0 copy-start.1
  0.7 0.0 copy-start.3
  0.7 0.0 copy-start.2
  0.7 5.0 %to_latitudes.1 = (bf16[16,8,1280]{2,1,0:T(8,128)(2,1)S(1)}, bf16[256,2560]{1,0:T(8,128)(2,1)S(1)}) custom-call(f32[8,32,640]{2,1,0:T(8,128)} %bitcast.7, bf16[8,640,640]{2,1,0:T(8,128)(2,1)} %legendre_ref.1), custom_call_target="tpu_custom_call" | custom-call | tf_op jit(solution)/shard_map/to_latitudes/pallas_call | solution.py:256
  5.7 0.0 copy-start.4
  5.7 22.3 %all_to_all.20 = bf16[16,8,1280]{2,1,0:T(8,128)(2,1)S(1)} all-to-all(bf16[16,8,1280]{2,1,0:T(8,128)(2,1)S(1)} %get-tuple-element.6), channel_id=1, replica_groups=mesh['member'=32,'wave'=16] {'wave'}, dimensions={0} | all-to-all | bytes 655360 | tf_op jit(solution)/shard_map/all_to_all | solution.py:272
  28.0 0.0 copy-done.3
  28.0 0.0 copy-done.2
  28.0 2.9 %on_grid.1 = bf16[128,1408]{1,0:T(8,128)(2,1)S(1)} custom-call(s32[4]{0:T(128)S(1)} %copy-done.3, bf16[128,1280]{1,0:T(8,128)(2,1)S(1)} %bitcast.10, bf16[256,2560]{1,0:T(8,128)(2,1)S(1)} %get-tuple-element.7.fourier_ref, f32[640]{0:T(1024)S(1)} %copy-done.2), custom_call_target="tpu_custom_call" | custom-call | tf_op jit(solution)/shard_map/on_grid/pallas_call | solution.py:275
  31.0 16.6 %all_to_all.21.coef_ref = bf16[16,8,1408]{2,1,0:T(8,128)(2,1)S(1)} all-to-all(bf16[16,8,1408]{2,1,0:T(8,128)(2,1)S(1)} %bitcast.9), channel_id=1, replica_groups=mesh['member'=32,'wave'=16] {'wave'}, dimensions={0} | all-to-all | bytes 720896 | tf_op jit(solution)/shard_map/all_to_all | solution.py:289
  47.6 0.0 copy-done
  47.6 0.0 copy-done.1
  47.6 3.1 %to_degrees.1 = (bf16[8,32,640]{2,1,0:T(8,128)(2,1)S(1)}, f32[1,1]{1,0:T(1,128)}) custom-call(s32[4]{0:T(128)S(1)} %copy-done.3, bf16[16,8,1408]{2,1,0:T(8,128)(2,1)S(1)} %all_to_all.21.coef_ref, bf16[8,640,640]{2,1,0:T(8,128)(2,1)S(1)} %copy-done, f32[8,32,640]{2,1,0:T(8,128)S(1)} %bitcast.8, f32[640]{0:T(1024)S(1)} %copy-done.2), custom_call_target="tpu_custom_call" | custom-call | tf_op jit(solution)/shard_map/to_degrees/pallas_call | solution.py:293
  50.7 25.8 %all_to_all.22.pieces_ref = bf16[32,8,640]{2,1,0:T(8,128)(2,1)S(1)} all-to-all(bf16[32,8,640]{2,1,0:T(8,128)(2,1)S(1)} %bitcast.11), channel_id=1, replica_groups=mesh['member'=32,'wave'=16] {'member'}, dimensions={0} | all-to-all | bytes 655360 | tf_op jit(solution)/shard_map/all_to_all | solution.py:309
  76.5 0.0 copy-done.4
  76.5 0.6 pick.1
  77.1 16.5 %all_to_all.23 = bf16[32,8,640]{2,1,0:T(8,128)(2,1)S(1)} all-to-all(bf16[32,8,640]{2,1,0:T(8,128)(2,1)S(1)} %pick.1), channel_id=1, replica_groups=mesh['member'=32,'wave'=16] {'member'}, dimensions={0} | all-to-all | bytes 655360 | tf_op jit(solution)/shard_map/all_to_all | solution.py:324
  93.6 0.9 convert.1
Async XLA Ops:
  0.6 46.9 %copy-start = (bf16[8,640,640]{2,1,0:T(8,128)(2,1)S(1)}, bf16[8,640,640]{2,1,0:T(8,128)(2,1)}, u32[]{:S(2)}) copy-start(bf16[8,640,640]{2,1,0:T(8,128)(2,1)} %legendre_ref.1) | copy-start | bytes 19660804
  0.6 46.9 %copy-start.1 = (f32[1,8,32,640]{3,2,1,0:T(8,128)S(1)}, f32[1,8,32,640]{3,2,1,0:T(8,128)}, u32[]{:S(2)}) copy-start(f32[1,8,32,640]{3,2,1,0:T(8,128)} %param.5) | copy-start | bytes 1966084
  0.7 27.4 %copy-start.3 = (s32[4]{0:T(128)S(1)}, s32[4]{0:T(128)}, u32[]{:S(2)}) copy-start(s32[4]{0:T(128)} %region_smem.3) | copy-start | bytes 52
  0.7 27.4 %copy-start.2 = (f32[640]{0:T(1024)S(1)}, f32[640]{0:T(1024)}, u32[]{:S(2)}) copy-start(f32[640]{0:T(1024)} %lat_weights_ref.3) | copy-start | bytes 7684
  5.7 70.9 %copy-start.4 = (s32[32]{0:T(128)S(1)}, s32[32]{0:T(128)}, u32[]{:S(2)}) copy-start(s32[32]{0:T(128)} %sources_smem.1) | copy-start | bytes 388

commit v4 on v3

--- a/solution.py
+++ b/solution.py
@@ -10,7 +10,7 @@
 NLON = 2560
 LANES = 128
 COLUMNS = 256
-AHEAD = 4
+AHEAD = 8
 
 advect_rate = 2.0
 
@@ -116,7 +116,6 @@
     weights_ref,
     turned_ref,
     total_ref,
-    region_ref,
 ):
     points = fourier_ref.shape[1]
     every = lat_weights_ref.shape[0]
@@ -125,38 +124,33 @@
     position = lax.axis_index("wave")
     lat_start = pl.multiple_of((position % 2) * lats, 8)
     weights_ref[...] = jnp.broadcast_to(lat_weights_ref[...].reshape(1, every), (8, every)).T
-    weights = weights_ref[pl.ds(lat_start, lats), 0:1]
+    weights = weights_ref[pl.ds(lat_start, lats), 0:1] * (synthesis_scale * synthesis_scale)
     for part in range(2):
         turned_ref[:, part * waves : (part + 1) * waves] = coef_ref[:, part * every : (part + 1) * every].T
-    total_ref[...] = jnp.zeros_like(total_ref)
-    region_ref[...] = jnp.zeros_like(region_ref)
+    region_sum = jnp.zeros((lats, LANES), jnp.float32)
     for part in range(points // COLUMNS):
         table = fourier_ref[:, part * COLUMNS : (part + 1) * COLUMNS]
-        grid = synthesis_scale * jnp.dot(
-            turned_ref[...], table, preferred_element_type=jnp.float32
-        )
+        grid = jnp.dot(turned_ref[...], table, preferred_element_type=jnp.float32)
         wind, temper = grid[:lats], grid[lats:]
         weighted = wind * weights
-        total_ref[:lats] += lax.dot_general(
-            (0.5 * wind * weighted).astype(jnp.bfloat16),
-            table,
-            (((1,), (1,)), ((), ())),
-            preferred_element_type=jnp.float32,
-        )
-        total_ref[lats:] += lax.dot_general(
-            (weighted * temper).astype(jnp.bfloat16),
-            table,
-            (((1,), (1,)), ((), ())),
-            preferred_element_type=jnp.float32,
-        )
+        for rows, flux in ((slice(0, lats), wind * weighted), (slice(lats, every), weighted * temper)):
+            term = lax.dot_general(
+                flux.astype(jnp.bfloat16),
+                table,
+                (((1,), (1,)), ((), ())),
+                preferred_element_type=jnp.float32,
+            )
+            total_ref[rows] = term if part == 0 else total_ref[rows] + term
         column = part * COLUMNS + lax.broadcasted_iota(jnp.int32, (1, COLUMNS), 1)
         inside = (column >= region_smem[2]) & (column < region_smem[3])
-        region_ref[...] += jnp.where(inside, temper * temper, 0.0)
+        squares = jnp.where(inside, temper * temper, 0.0)
+        for tile in range(COLUMNS // LANES):
+            region_sum += squares[:, tile * LANES : (tile + 1) * LANES]
     lat = lat_start + lax.broadcasted_iota(jnp.int32, (lats, 1), 0)
     lowest = position // 2 == levels - 1
     lat_inside = (lat >= region_smem[0]) & (lat < region_smem[1]) & lowest
     score = jnp.sum(
-        jnp.where(lat_inside, weights, 0.0) * jnp.sum(region_ref[...], axis=1, keepdims=True),
+        jnp.where(lat_inside, weights, 0.0) * jnp.sum(region_sum, axis=1, keepdims=True),
         axis=0,
         keepdims=True,
     )
@@ -167,9 +161,11 @@
     lane = lax.broadcasted_iota(jnp.int32, score.shape, 1)
     parts = jnp.where(lane == 0, high, jnp.where(lane == 1, middle, jnp.where(lane == 2, low, 0.0)))
     out_ref[:, 2 * every :] = parts.astype(jnp.bfloat16)
+    row = lax.broadcasted_iota(jnp.int32, (every, 1), 0)
+    scale = jnp.where(row < lats, 0.5 * analysis_scale, analysis_scale)
     for part in range(2):
         out_ref[:, part * every : (part + 1) * every] = (
-            (analysis_scale * total_ref[:, part * waves : (part + 1) * waves]).T.astype(jnp.bfloat16)
+            (scale * total_ref[:, part * waves : (part + 1) * waves]).astype(jnp.bfloat16).T
         )
 
 
@@ -202,7 +198,7 @@
 
     position = lax.axis_index("wave")
     degree = lax.broadcasted_iota(jnp.int32, (1, degrees), 1).astype(jnp.float32)
-    damping = 1.0 + ((degree + 1.0) / degrees) ** 2
+    undamped = 1.0 / (1.0 + ((degree + 1.0) / degrees) ** 2)
     left = lax.broadcasted_iota(jnp.int32, (levels, lats), 1) < half
     middle = 2 * levels
     for wave in range(waves):
@@ -221,10 +217,10 @@
         global_wave = (position * waves + wave).astype(jnp.float32)
         advection = advect_rate * global_wave / waves_total
         out_ref[wave, :middle] = (
-            (state_ref[wave, :middle] + advection * tendency[middle:]) / damping
+            (state_ref[wave, :middle] + advection * tendency[middle:]) * undamped
         ).astype(jnp.bfloat16)
         out_ref[wave, middle:] = (
-            (state_ref[wave, middle:] - advection * tendency[:middle]) / damping
+            (state_ref[wave, middle:] - advection * tendency[:middle]) * undamped
         ).astype(jnp.bfloat16)
 
 
@@ -240,29 +236,29 @@
     waves_total = waves_local * wave_count
     state_rows = state.shape[2]
     levels = state_rows // 4
-    half = latitudes // 2
     spectral = state[0]
     lat_row = lat_weights
     whole = pl.BlockSpec(memory_space=pltpu.VMEM)
     scalars = pl.BlockSpec(memory_space=pltpu.SMEM)
     stay = pl.BlockSpec(memory_space=pltpu.HBM)
-    small = pltpu.CompilerParams(vmem_limit_bytes=24 << 20)
+    small = pltpu.CompilerParams(vmem_limit_bytes=16 << 20)
     near = [
         pltpu.VMEM(legendre.shape, jnp.bfloat16),
         pltpu.VMEM(spectral.shape, jnp.float32),
     ]
     arrivals = [pltpu.SemaphoreType.DMA((waves_local,)), pltpu.SemaphoreType.DMA((waves_local,))]
 
-    coef, fourier = pl.pallas_call(
+    coef, fourier, legendre_near = pl.pallas_call(
         functools.partial(to_latitudes, levels),
         in_specs=[stay, stay],
-        out_specs=[whole, whole],
+        out_specs=[whole, whole, whole],
         out_shape=[
-            jax.ShapeDtypeStruct((wave_count, waves_local, 2 * latitudes), jnp.bfloat16),
+            pltpu.VMEM((wave_count, waves_local, 2 * latitudes), jnp.bfloat16),
             pltpu.VMEM((2 * waves_total, NLON), jnp.bfloat16),
+            pltpu.VMEM(legendre.shape, jnp.bfloat16),
         ],
         scratch_shapes=[
-            *near,
+            pltpu.VMEM(spectral.shape, jnp.float32),
             pltpu.VMEM((latitudes // LANES, waves_local * state_rows, LANES), jnp.float32),
             *arrivals,
         ],
@@ -281,7 +277,6 @@
             pltpu.VMEM((latitudes, 8), jnp.float32),
             pltpu.VMEM((latitudes, 2 * waves_total), jnp.bfloat16),
             pltpu.VMEM((latitudes, 2 * waves_total), jnp.float32),
-            pltpu.VMEM((half, COLUMNS), jnp.float32),
         ],
         compiler_params=small,
         name="on_grid",
@@ -303,7 +298,7 @@
         ],
         compiler_params=small,
         name="to_degrees",
-    )(region, flux_coef, legendre, spectral, lat_row)
+    )(region, flux_coef, legendre_near, spectral, lat_row)
 
     piece_rows = waves_local * state_rows // member_count
     pieces = lax.all_to_all(

time: 94.7 us -> 93.6 us (0.988)
  Pallas kernels: 11.6 us -> 10.5 us
    pallas_call x1, Pallas kernels: 4.97 us -> 3.97 us  [on_device(): pl.pallas_call(functools.partial(to_latitudes, levels), in_specs=[stay, s...]
where the time goes in v4:
time: 93.6 us; the launch traced here: 93.3 us
  blocking collectives  81.2 us (87%)
  Pallas kernels  10.5 us (11%)
    all_to_all x1, blocking collectives, on_device(): lax.all_to_all(stepped.reshape(member_count, piece_rows, degrees), 'membe...  25.8 us
    all_to_all x1, blocking collectives, on_device(): coef = lax.all_to_all(coef, 'wave', split_axis=0, concat_axis=0, tiled=True)  22.3 us
    all_to_all x1, blocking collectives, on_device(): lax.all_to_all(flux_coef.reshape(wave_count, waves_local, width), 'wave',...  16.6 us
    all_to_all x1, blocking collectives, on_device(): lax.all_to_all(picked, 'member', split_axis=0, concat_axis=0, tiled=True)  16.5 us
    pallas_call x1, Pallas kernels, on_device(): pl.pallas_call(functools.partial(to_latitudes, levels), in_specs=[stay, s...  3.97 us
    pallas_call x1, Pallas kernels, on_device(): pl.pallas_call(functools.partial(to_degrees, levels, waves_total), in_spe...  3.11 us
    pallas_call x1, Pallas kernels, on_device(): pl.pallas_call(functools.partial(on_grid, (2.0 * waves_total) ** (-0.5),...  2.86 us

profile of v4, /device:TPU:1, one launch (start us, length us, event | category | flops | bytes accessed | tf_op | source)
XLA Modules:
  0.0 93.3 jit_solution(4569094822988019168)
XLA Ops:
  0.6 0.0 copy-start
  0.6 0.0 copy-start.2
  0.7 0.0 copy-start.1
  0.7 4.0 %to_latitudes.1 = (bf16[16,8,1280]{2,1,0:T(8,128)(2,1)S(1)}, bf16[256,2560]{1,0:T(8,128)(2,1)S(1)}, bf16[8,640,640]{2,1,0:T(8,128)(2,1)S(1)}) custom-call(f32[8,32,640]{2,1,0:T(8,128)} %bitcast.7, bf16[8,640,640]{2,1,0:T(8,128)(2,1)} %legendre_hbm.1), custom_call_target="tpu_custom_call" | custom-call | tf_op jit(solution)/shard_map/to_latitudes/pallas_call | solution.py:251
  4.6 0.0 copy-start.3
  4.6 22.3 %all_to_all.20 = bf16[16,8,1280]{2,1,0:T(8,128)(2,1)S(1)} all-to-all(bf16[16,8,1280]{2,1,0:T(8,128)(2,1)S(1)} %get-tuple-element.7), channel_id=1, replica_groups=mesh['member'=32,'wave'=16] {'wave'}, dimensions={0} | all-to-all | bytes 655360 | tf_op jit(solution)/shard_map/all_to_all | solution.py:268
  27.0 0.0 copy-done.2
  27.0 0.0 copy-done.1
  27.0 2.9 %on_grid.1 = bf16[128,1408]{1,0:T(8,128)(2,1)S(1)} custom-call(s32[4]{0:T(128)S(1)} %copy-done.2, bf16[128,1280]{1,0:T(8,128)(2,1)S(1)} %bitcast.10, bf16[256,2560]{1,0:T(8,128)(2,1)S(1)} %get-tuple-element.8.fourier_ref, f32[640]{0:T(1024)S(1)} %copy-done.1), custom_call_target="tpu_custom_call" | custom-call | tf_op jit(solution)/shard_map/on_grid/pallas_call | solution.py:271
  29.8 16.6 %all_to_all.21.coef_ref = bf16[16,8,1408]{2,1,0:T(8,128)(2,1)S(1)} all-to-all(bf16[16,8,1408]{2,1,0:T(8,128)(2,1)S(1)} %bitcast.9), channel_id=1, replica_groups=mesh['member'=32,'wave'=16] {'wave'}, dimensions={0} | all-to-all | bytes 720896 | tf_op jit(solution)/shard_map/all_to_all | solution.py:284
  46.5 0.0 copy-done
  46.5 3.1 %to_degrees.1 = (bf16[8,32,640]{2,1,0:T(8,128)(2,1)S(1)}, f32[1,1]{1,0:T(1,128)}) custom-call(s32[4]{0:T(128)S(1)} %copy-done.2, bf16[16,8,1408]{2,1,0:T(8,128)(2,1)S(1)} %all_to_all.21.coef_ref, bf16[8,640,640]{2,1,0:T(8,128)(2,1)S(1)} %get-tuple-element.9.legendre_ref, f32[8,32,640]{2,1,0:T(8,128)S(1)} %bitcast.8, f32[640]{0:T(1024)S(1)} %copy-done.1), custom_call_target="tpu_custom_call" | custom-call | tf_op jit(solution)/shard_map/to_degrees/pallas_call | solution.py:288
  49.6 25.8 %all_to_all.22.pieces_ref = bf16[32,8,640]{2,1,0:T(8,128)(2,1)S(1)} all-to-all(bf16[32,8,640]{2,1,0:T(8,128)(2,1)S(1)} %bitcast.11), channel_id=1, replica_groups=mesh['member'=32,'wave'=16] {'member'}, dimensions={0} | all-to-all | bytes 655360 | tf_op jit(solution)/shard_map/all_to_all | solution.py:304
  75.4 0.0 copy-done.3
  75.4 0.6 pick.1
  76.0 16.5 %all_to_all.23 = bf16[32,8,640]{2,1,0:T(8,128)(2,1)S(1)} all-to-all(bf16[32,8,640]{2,1,0:T(8,128)(2,1)S(1)} %pick.1), channel_id=1, replica_groups=mesh['member'=32,'wave'=16] {'member'}, dimensions={0} | all-to-all | bytes 655360 | tf_op jit(solution)/shard_map/all_to_all | solution.py:319
  92.5 0.9 convert.1
Async XLA Ops:
  0.6 45.8 %copy-start = (f32[1,8,32,640]{3,2,1,0:T(8,128)S(1)}, f32[1,8,32,640]{3,2,1,0:T(8,128)}, u32[]{:S(2)}) copy-start(f32[1,8,32,640]{3,2,1,0:T(8,128)} %param.5) | copy-start | bytes 1966084
  0.6 26.3 %copy-start.2 = (s32[4]{0:T(128)S(1)}, s32[4]{0:T(128)}, u32[]{:S(2)}) copy-start(s32[4]{0:T(128)} %region_smem.3) | copy-start | bytes 52
  0.7 26.3 %copy-start.1 = (f32[640]{0:T(1024)S(1)}, f32[640]{0:T(1024)}, u32[]{:S(2)}) copy-start(f32[640]{0:T(1024)} %lat_weights_ref.3) | copy-start | bytes 7684
  4.6 70.8 %copy-start.3 = (s32[32]{0:T(128)S(1)}, s32[32]{0:T(128)}, u32[]{:S(2)}) copy-start(s32[32]{0:T(128)} %sources_smem.1) | copy-start | bytes 388

commit v5 on v4

--- a/solution.py
+++ b/solution.py
@@ -80,7 +80,7 @@
             legendre_ref[wave],
             preferred_element_type=jnp.float32,
         )
-        put_rows(rows_ref, 0, pl.ds(wave * rows, rows), product)
+        put_rows(rows_ref, 0, pl.ds(wave, rows, stride=waves), product)
         for tile in range(wave * tiles // waves, (wave + 1) * tiles // waves):
             for part in range(2):
                 here = slice(part * total, (part + 1) * total)
@@ -95,8 +95,8 @@
     for level in range(levels):
         for part in range(2):
             first = 2 * levels * part + level
-            wind = get_rows(rows_ref, 0, span, pl.ds(first, waves, stride=rows))
-            temper = get_rows(rows_ref, 0, span, pl.ds(first + levels, waves, stride=rows))
+            wind = get_rows(rows_ref, 0, span, pl.ds(first * waves, waves))
+            temper = get_rows(rows_ref, 0, span, pl.ds((first + levels) * waves, waves))
             low = jnp.where(left, wind, pltpu.roll(temper, half, 1))
             high = jnp.where(left, pltpu.roll(wind, half, 1), temper)
             here = slice(part * width, (part + 1) * width)
@@ -209,11 +209,11 @@
             rows.append(jnp.where(left, first, pltpu.roll(second, half, 1)))
             rows.append(jnp.where(left, pltpu.roll(first, half, 1), second))
         tendency = lax.dot_general(
+            legendre_ref[wave],
             jnp.concatenate(rows, axis=0).astype(jnp.bfloat16),
-            legendre_ref[wave],
             (((1,), (1,)), ((), ())),
             preferred_element_type=jnp.float32,
-        )
+        ).T
         global_wave = (position * waves + wave).astype(jnp.float32)
         advection = advect_rate * global_wave / waves_total
         out_ref[wave, :middle] = (

time: 93.6 us -> 93.2 us (level)
  no operation moved by 1% of the time
where the time goes in v5:
time: 93.2 us; the launch traced here: 93 us
  blocking collectives  81.2 us (87%)
  Pallas kernels  10.1 us (11%)
    all_to_all x1, blocking collectives, on_device(): lax.all_to_all(stepped.reshape(member_count, piece_rows, degrees), 'membe...  25.8 us
    all_to_all x1, blocking collectives, on_device(): coef = lax.all_to_all(coef, 'wave', split_axis=0, concat_axis=0, tiled=True)  22.3 us
    all_to_all x1, blocking collectives, on_device(): lax.all_to_all(flux_coef.reshape(wave_count, waves_local, width), 'wave',...  16.6 us
    all_to_all x1, blocking collectives, on_device(): lax.all_to_all(picked, 'member', split_axis=0, concat_axis=0, tiled=True)  16.5 us
    pallas_call x1, Pallas kernels, on_device(): pl.pallas_call(functools.partial(to_latitudes, levels), in_specs=[stay, s...  3.8 us
    pallas_call x1, Pallas kernels, on_device(): pl.pallas_call(functools.partial(to_degrees, levels, waves_total), in_spe...  2.9 us
    pallas_call x1, Pallas kernels, on_device(): pl.pallas_call(functools.partial(on_grid, (2.0 * waves_total) ** (-0.5),...  2.86 us

profile of v5, /device:TPU:1, one launch (start us, length us, event | category | flops | bytes accessed | tf_op | source)
XLA Modules:
  0.0 93.0 jit_solution(13917780167163650645)
XLA Ops:
  0.6 0.0 copy-start
  0.6 0.0 copy-start.2
  0.7 0.0 copy-start.1
  0.7 3.8 %to_latitudes.1 = (bf16[16,8,1280]{2,1,0:T(8,128)(2,1)S(1)}, bf16[256,2560]{1,0:T(8,128)(2,1)S(1)}, bf16[8,640,640]{2,1,0:T(8,128)(2,1)S(1)}) custom-call(f32[8,32,640]{2,1,0:T(8,128)} %bitcast.7, bf16[8,640,640]{2,1,0:T(8,128)(2,1)} %legendre_hbm.1), custom_call_target="tpu_custom_call" | custom-call | tf_op jit(solution)/shard_map/to_latitudes/pallas_call | solution.py:251
  4.5 0.0 copy-start.3
  4.5 22.3 %all_to_all.20 = bf16[16,8,1280]{2,1,0:T(8,128)(2,1)S(1)} all-to-all(bf16[16,8,1280]{2,1,0:T(8,128)(2,1)S(1)} %get-tuple-element.7), channel_id=1, replica_groups=mesh['member'=32,'wave'=16] {'wave'}, dimensions={0} | all-to-all | bytes 655360 | tf_op jit(solution)/shard_map/all_to_all | solution.py:268
  26.8 0.0 copy-done.2
  26.8 0.0 copy-done.1
  26.8 2.9 %on_grid.1 = bf16[128,1408]{1,0:T(8,128)(2,1)S(1)} custom-call(s32[4]{0:T(128)S(1)} %copy-done.2, bf16[128,1280]{1,0:T(8,128)(2,1)S(1)} %bitcast.10, bf16[256,2560]{1,0:T(8,128)(2,1)S(1)} %get-tuple-element.8.fourier_ref, f32[640]{0:T(1024)S(1)} %copy-done.1), custom_call_target="tpu_custom_call" | custom-call | tf_op jit(solution)/shard_map/on_grid/pallas_call | solution.py:271
  29.7 16.6 %all_to_all.21.coef_ref = bf16[16,8,1408]{2,1,0:T(8,128)(2,1)S(1)} all-to-all(bf16[16,8,1408]{2,1,0:T(8,128)(2,1)S(1)} %bitcast.9), channel_id=1, replica_groups=mesh['member'=32,'wave'=16] {'wave'}, dimensions={0} | all-to-all | bytes 720896 | tf_op jit(solution)/shard_map/all_to_all | solution.py:284
  46.3 0.0 copy-done
  46.3 2.9 %to_degrees.1 = (bf16[8,32,640]{2,1,0:T(8,128)(2,1)S(1)}, f32[1,1]{1,0:T(1,128)}) custom-call(s32[4]{0:T(128)S(1)} %copy-done.2, bf16[16,8,1408]{2,1,0:T(8,128)(2,1)S(1)} %all_to_all.21.coef_ref, bf16[8,640,640]{2,1,0:T(8,128)(2,1)S(1)} %get-tuple-element.9.legendre_ref, f32[8,32,640]{2,1,0:T(8,128)S(1)} %bitcast.8, f32[640]{0:T(1024)S(1)} %copy-done.1), custom_call_target="tpu_custom_call" | custom-call | tf_op jit(solution)/shard_map/to_degrees/pallas_call | solution.py:288
  49.2 25.8 %all_to_all.22.pieces_ref = bf16[32,8,640]{2,1,0:T(8,128)(2,1)S(1)} all-to-all(bf16[32,8,640]{2,1,0:T(8,128)(2,1)S(1)} %bitcast.11), channel_id=1, replica_groups=mesh['member'=32,'wave'=16] {'member'}, dimensions={0} | all-to-all | bytes 655360 | tf_op jit(solution)/shard_map/all_to_all | solution.py:304
  75.0 0.0 copy-done.3
  75.0 0.6 pick.1
  75.6 16.5 %all_to_all.23 = bf16[32,8,640]{2,1,0:T(8,128)(2,1)S(1)} all-to-all(bf16[32,8,640]{2,1,0:T(8,128)(2,1)S(1)} %pick.1), channel_id=1, replica_groups=mesh['member'=32,'wave'=16] {'member'}, dimensions={0} | all-to-all | bytes 655360 | tf_op jit(solution)/shard_map/all_to_all | solution.py:319
  92.1 0.9 convert.1
Async XLA Ops:
  0.6 45.7 %copy-start = (f32[1,8,32,640]{3,2,1,0:T(8,128)S(1)}, f32[1,8,32,640]{3,2,1,0:T(8,128)}, u32[]{:S(2)}) copy-start(f32[1,8,32,640]{3,2,1,0:T(8,128)} %param.5) | copy-start | bytes 1966084
  0.6 26.2 %copy-start.2 = (s32[4]{0:T(128)S(1)}, s32[4]{0:T(128)}, u32[]{:S(2)}) copy-start(s32[4]{0:T(128)} %region_smem.3) | copy-start | bytes 52
  0.7 26.2 %copy-start.1 = (f32[640]{0:T(1024)S(1)}, f32[640]{0:T(1024)}, u32[]{:S(2)}) copy-start(f32[640]{0:T(1024)} %lat_weights_ref.3) | copy-start | bytes 7684
  4.5 70.6 %copy-start.3 = (s32[32]{0:T(128)S(1)}, s32[32]{0:T(128)}, u32[]{:S(2)}) copy-start(s32[32]{0:T(128)} %sources_smem.1) | copy-start | bytes 388

commit v6 on v5

--- a/solution.py
+++ b/solution.py
@@ -248,17 +248,17 @@
     ]
     arrivals = [pltpu.SemaphoreType.DMA((waves_local,)), pltpu.SemaphoreType.DMA((waves_local,))]
 
-    coef, fourier, legendre_near = pl.pallas_call(
+    coef, fourier, legendre_near, spectral_near = pl.pallas_call(
         functools.partial(to_latitudes, levels),
         in_specs=[stay, stay],
-        out_specs=[whole, whole, whole],
+        out_specs=[whole, whole, whole, whole],
         out_shape=[
             pltpu.VMEM((wave_count, waves_local, 2 * latitudes), jnp.bfloat16),
             pltpu.VMEM((2 * waves_total, NLON), jnp.bfloat16),
             pltpu.VMEM(legendre.shape, jnp.bfloat16),
+            pltpu.VMEM(spectral.shape, jnp.float32),
         ],
         scratch_shapes=[
-            pltpu.VMEM(spectral.shape, jnp.float32),
             pltpu.VMEM((latitudes // LANES, waves_local * state_rows, LANES), jnp.float32),
             *arrivals,
         ],
@@ -298,7 +298,7 @@
         ],
         compiler_params=small,
         name="to_degrees",
-    )(region, flux_coef, legendre_near, spectral, lat_row)
+    )(region, flux_coef, legendre_near, spectral_near, lat_row)
 
     piece_rows = waves_local * state_rows // member_count
     pieces = lax.all_to_all(

time: 93.2 us -> 93.2 us (level)
  no operation moved by 1% of the time
where the time goes in v6:
time: 93.2 us; the launch traced here: 92.9 us
  blocking collectives  81.2 us (87%)
  Pallas kernels  10.1 us (11%)
    all_to_all x1, blocking collectives, on_device(): lax.all_to_all(stepped.reshape(member_count, piece_rows, degrees), 'membe...  25.8 us
    all_to_all x1, blocking collectives, on_device(): coef = lax.all_to_all(coef, 'wave', split_axis=0, concat_axis=0, tiled=True)  22.3 us
    all_to_all x1, blocking collectives, on_device(): lax.all_to_all(flux_coef.reshape(wave_count, waves_local, width), 'wave',...  16.6 us
    all_to_all x1, blocking collectives, on_device(): lax.all_to_all(picked, 'member', split_axis=0, concat_axis=0, tiled=True)  16.5 us
    pallas_call x1, Pallas kernels, on_device(): pl.pallas_call(functools.partial(to_latitudes, levels), in_specs=[stay, s...  3.76 us
    pallas_call x1, Pallas kernels, on_device(): pl.pallas_call(functools.partial(to_degrees, levels, waves_total), in_spe...  2.9 us
    pallas_call x1, Pallas kernels, on_device(): pl.pallas_call(functools.partial(on_grid, (2.0 * waves_total) ** (-0.5),...  2.86 us

profile of v6, /device:TPU:1, one launch (start us, length us, event | category | flops | bytes accessed | tf_op | source)
XLA Modules:
  0.0 92.9 jit_solution(13958778945282607462)
XLA Ops:
  0.6 0.0 copy-start.1
  0.6 0.0 copy-start
  0.7 3.8 %to_latitudes.1 = (bf16[16,8,1280]{2,1,0:T(8,128)(2,1)S(1)}, bf16[256,2560]{1,0:T(8,128)(2,1)S(1)}, bf16[8,640,640]{2,1,0:T(8,128)(2,1)S(1)}, f32[8,32,640]{2,1,0:T(8,128)S(1)}) custom-call(f32[8,32,640]{2,1,0:T(8,128)} %bitcast.11, bf16[8,640,640]{2,1,0:T(8,128)(2,1)} %legendre_hbm.1), custom_call_target="tpu_custom_call" | custom-call | tf_op jit(solution)/shard_map/to_latitudes/pallas_call | solution.py:251
  4.4 0.0 copy-start.2
  4.4 22.3 %all_to_all.20 = bf16[16,8,1280]{2,1,0:T(8,128)(2,1)S(1)} all-to-all(bf16[16,8,1280]{2,1,0:T(8,128)(2,1)S(1)} %get-tuple-element.8), channel_id=1, replica_groups=mesh['member'=32,'wave'=16] {'wave'}, dimensions={0} | all-to-all | bytes 655360 | tf_op jit(solution)/shard_map/all_to_all | solution.py:268
  26.8 0.0 copy-done.1
  26.8 0.0 copy-done
  26.8 2.9 %on_grid.1 = bf16[128,1408]{1,0:T(8,128)(2,1)S(1)} custom-call(s32[4]{0:T(128)S(1)} %copy-done.1, bf16[128,1280]{1,0:T(8,128)(2,1)S(1)} %bitcast.8, bf16[256,2560]{1,0:T(8,128)(2,1)S(1)} %get-tuple-element.9.fourier_ref, f32[640]{0:T(1024)S(1)} %copy-done), custom_call_target="tpu_custom_call" | custom-call | tf_op jit(solution)/shard_map/on_grid/pallas_call | solution.py:271
  29.6 16.6 %all_to_all.21.coef_ref = bf16[16,8,1408]{2,1,0:T(8,128)(2,1)S(1)} all-to-all(bf16[16,8,1408]{2,1,0:T(8,128)(2,1)S(1)} %bitcast.7), channel_id=1, replica_groups=mesh['member'=32,'wave'=16] {'wave'}, dimensions={0} | all-to-all | bytes 720896 | tf_op jit(solution)/shard_map/all_to_all | solution.py:284
  46.2 2.9 %to_degrees.1 = (bf16[8,32,640]{2,1,0:T(8,128)(2,1)S(1)}, f32[1,1]{1,0:T(1,128)}) custom-call(s32[4]{0:T(128)S(1)} %copy-done.1, bf16[16,8,1408]{2,1,0:T(8,128)(2,1)S(1)} %all_to_all.21.coef_ref, bf16[8,640,640]{2,1,0:T(8,128)(2,1)S(1)} %get-tuple-element.10.legendre_ref, f32[8,32,640]{2,1,0:T(8,128)S(1)} %get-tuple-element.11.state_ref, f32[640]{0:T(1024)S(1)} %copy-done), custom_call_target="tpu_custom_call" | custom-call | tf_op jit(solution)/shard_map/to_degrees/pallas_call | solution.py:288
  49.2 25.8 %all_to_all.22.pieces_ref = bf16[32,8,640]{2,1,0:T(8,128)(2,1)S(1)} all-to-all(bf16[32,8,640]{2,1,0:T(8,128)(2,1)S(1)} %bitcast.9), channel_id=1, replica_groups=mesh['member'=32,'wave'=16] {'member'}, dimensions={0} | all-to-all | bytes 655360 | tf_op jit(solution)/shard_map/all_to_all | solution.py:304
  75.0 0.0 copy-done.2
  75.0 0.6 pick.1
  75.6 16.5 %all_to_all.23 = bf16[32,8,640]{2,1,0:T(8,128)(2,1)S(1)} all-to-all(bf16[32,8,640]{2,1,0:T(8,128)(2,1)S(1)} %pick.1), channel_id=1, replica_groups=mesh['member'=32,'wave'=16] {'member'}, dimensions={0} | all-to-all | bytes 655360 | tf_op jit(solution)/shard_map/all_to_all | solution.py:319
  92.0 0.9 convert.1
Async XLA Ops:
  0.6 26.1 %copy-start.1 = (s32[4]{0:T(128)S(1)}, s32[4]{0:T(128)}, u32[]{:S(2)}) copy-start(s32[4]{0:T(128)} %region_smem.3) | copy-start | bytes 52
  0.6 26.1 %copy-start = (f32[640]{0:T(1024)S(1)}, f32[640]{0:T(1024)}, u32[]{:S(2)}) copy-start(f32[640]{0:T(1024)} %lat_weights_ref.3) | copy-start | bytes 7684
  4.4 70.6 %copy-start.2 = (s32[32]{0:T(128)S(1)}, s32[32]{0:T(128)}, u32[]{:S(2)}) copy-start(s32[32]{0:T(128)} %sources_smem.1) | copy-start | bytes 388

commit v7 on v5

--- a/solution.py
+++ b/solution.py
@@ -61,7 +61,15 @@
     legendre_sems,
 ):
     waves, rows, _ = state_hbm.shape
-    copies = routes(waves, (state_hbm, state_ref, state_sems), (legendre_hbm, legendre_ref, legendre_sems))
+    halves = [pl.ds(part * (legendre_hbm.shape[1] // 2), legendre_hbm.shape[1] // 2) for part in range(2)]
+    copies = routes(
+        waves,
+        (state_hbm, state_ref, state_sems),
+        *(
+            (legendre_hbm.at[:, here], legendre_ref.at[:, here], legendre_sems.at[part])
+            for part, here in enumerate(halves)
+        ),
+    )
     table_rows, points = fourier_ref.shape
     total = table_rows // 2
     row = lax.broadcasted_iota(jnp.int32, (table_rows, LANES), 0)
@@ -246,7 +254,7 @@
         pltpu.VMEM(legendre.shape, jnp.bfloat16),
         pltpu.VMEM(spectral.shape, jnp.float32),
     ]
-    arrivals = [pltpu.SemaphoreType.DMA((waves_local,)), pltpu.SemaphoreType.DMA((waves_local,))]
+    arrivals = [pltpu.SemaphoreType.DMA((waves_local,)), pltpu.SemaphoreType.DMA((2, waves_local))]
 
     coef, fourier, legendre_near = pl.pallas_call(
         functools.partial(to_latitudes, levels),

time: 93.2 us -> 94.8 us (1.017)
  Pallas kernels: 10.1 us -> 11.6 us
    pallas_call x1, Pallas kernels: 3.8 us -> 5.3 us  [on_device(): pl.pallas_call(functools.partial(to_latitudes, levels), in_specs=[stay, s...]
where the time goes in v7:
time: 94.8 us; the launch traced here: 94.5 us
  blocking collectives  81.3 us (86%)
  Pallas kernels  11.6 us (12%)
    all_to_all x1, blocking collectives, on_device(): lax.all_to_all(stepped.reshape(member_count, piece_rows, degrees), 'membe...  25.8 us
    all_to_all x1, blocking collectives, on_device(): coef = lax.all_to_all(coef, 'wave', split_axis=0, concat_axis=0, tiled=True)  22.3 us
    all_to_all x1, blocking collectives, on_device(): lax.all_to_all(flux_coef.reshape(wave_count, waves_local, width), 'wave',...  16.6 us
    all_to_all x1, blocking collectives, on_device(): lax.all_to_all(picked, 'member', split_axis=0, concat_axis=0, tiled=True)  16.5 us
    pallas_call x1, Pallas kernels, on_device(): pl.pallas_call(functools.partial(to_latitudes, levels), in_specs=[stay, s...  5.3 us
    pallas_call x1, Pallas kernels, on_device(): pl.pallas_call(functools.partial(to_degrees, levels, waves_total), in_spe...  2.9 us
    pallas_call x1, Pallas kernels, on_device(): pl.pallas_call(functools.partial(on_grid, (2.0 * waves_total) ** (-0.5),...  2.86 us

profile of v7, /device:TPU:1, one launch (start us, length us, event | category | flops | bytes accessed | tf_op | source)
XLA Modules:
  0.0 94.5 jit_solution(912692614924121377)
XLA Ops:
  0.6 0.0 copy-start
  0.6 0.0 copy-start.2
  0.7 0.0 copy-start.1
  0.7 5.3 %to_latitudes.1 = (bf16[16,8,1280]{2,1,0:T(8,128)(2,1)S(1)}, bf16[256,2560]{1,0:T(8,128)(2,1)S(1)}, bf16[8,640,640]{2,1,0:T(8,128)(2,1)S(1)}) custom-call(f32[8,32,640]{2,1,0:T(8,128)} %bitcast.7, bf16[8,640,640]{2,1,0:T(8,128)(2,1)} %legendre_hbm.1), custom_call_target="tpu_custom_call" | custom-call | tf_op jit(solution)/shard_map/to_latitudes/pallas_call | solution.py:259
  6.0 0.0 copy-start.3
  6.0 22.3 %all_to_all.20 = bf16[16,8,1280]{2,1,0:T(8,128)(2,1)S(1)} all-to-all(bf16[16,8,1280]{2,1,0:T(8,128)(2,1)S(1)} %get-tuple-element.7), channel_id=1, replica_groups=mesh['member'=32,'wave'=16] {'wave'}, dimensions={0} | all-to-all | bytes 655360 | tf_op jit(solution)/shard_map/all_to_all | solution.py:276
  28.3 0.0 copy-done.2
  28.3 0.0 copy-done.1
  28.3 2.9 %on_grid.1 = bf16[128,1408]{1,0:T(8,128)(2,1)S(1)} custom-call(s32[4]{0:T(128)S(1)} %copy-done.2, bf16[128,1280]{1,0:T(8,128)(2,1)S(1)} %bitcast.10, bf16[256,2560]{1,0:T(8,128)(2,1)S(1)} %get-tuple-element.8.fourier_ref, f32[640]{0:T(1024)S(1)} %copy-done.1), custom_call_target="tpu_custom_call" | custom-call | tf_op jit(solution)/shard_map/on_grid/pallas_call | solution.py:279
  31.2 16.6 %all_to_all.21.coef_ref = bf16[16,8,1408]{2,1,0:T(8,128)(2,1)S(1)} all-to-all(bf16[16,8,1408]{2,1,0:T(8,128)(2,1)S(1)} %bitcast.9), channel_id=1, replica_groups=mesh['member'=32,'wave'=16] {'wave'}, dimensions={0} | all-to-all | bytes 720896 | tf_op jit(solution)/shard_map/all_to_all | solution.py:292
  47.8 0.0 copy-done
  47.8 2.9 %to_degrees.1 = (bf16[8,32,640]{2,1,0:T(8,128)(2,1)S(1)}, f32[1,1]{1,0:T(1,128)}) custom-call(s32[4]{0:T(128)S(1)} %copy-done.2, bf16[16,8,1408]{2,1,0:T(8,128)(2,1)S(1)} %all_to_all.21.coef_ref, bf16[8,640,640]{2,1,0:T(8,128)(2,1)S(1)} %get-tuple-element.9.legendre_ref, f32[8,32,640]{2,1,0:T(8,128)S(1)} %bitcast.8, f32[640]{0:T(1024)S(1)} %copy-done.1), custom_call_target="tpu_custom_call" | custom-call | tf_op jit(solution)/shard_map/to_degrees/pallas_call | solution.py:296
  50.7 25.8 %all_to_all.22.pieces_ref = bf16[32,8,640]{2,1,0:T(8,128)(2,1)S(1)} all-to-all(bf16[32,8,640]{2,1,0:T(8,128)(2,1)S(1)} %bitcast.11), channel_id=1, replica_groups=mesh['member'=32,'wave'=16] {'member'}, dimensions={0} | all-to-all | bytes 655360 | tf_op jit(solution)/shard_map/all_to_all | solution.py:312
  76.5 0.0 copy-done.3
  76.5 0.6 pick.1
  77.1 16.5 %all_to_all.23 = bf16[32,8,640]{2,1,0:T(8,128)(2,1)S(1)} all-to-all(bf16[32,8,640]{2,1,0:T(8,128)(2,1)S(1)} %pick.1), channel_id=1, replica_groups=mesh['member'=32,'wave'=16] {'member'}, dimensions={0} | all-to-all | bytes 655360 | tf_op jit(solution)/shard_map/all_to_all | solution.py:327
  93.6 0.9 convert.1
Async XLA Ops:
  0.6 47.2 %copy-start = (f32[1,8,32,640]{3,2,1,0:T(8,128)S(1)}, f32[1,8,32,640]{3,2,1,0:T(8,128)}, u32[]{:S(2)}) copy-start(f32[1,8,32,640]{3,2,1,0:T(8,128)} %param.5) | copy-start | bytes 1966084
  0.6 27.7 %copy-start.2 = (s32[4]{0:T(128)S(1)}, s32[4]{0:T(128)}, u32[]{:S(2)}) copy-start(s32[4]{0:T(128)} %region_smem.3) | copy-start | bytes 52
  0.7 27.7 %copy-start.1 = (f32[640]{0:T(1024)S(1)}, f32[640]{0:T(1024)}, u32[]{:S(2)}) copy-start(f32[640]{0:T(1024)} %lat_weights_ref.3) | copy-start | bytes 7684
  6.0 70.6 %copy-start.3 = (s32[32]{0:T(128)S(1)}, s32[32]{0:T(128)}, u32[]{:S(2)}) copy-start(s32[32]{0:T(128)} %sources_smem.1) | copy-start | bytes 388
